TPU v7x, 256 devices: a whole 4x4x8 slice. The times are simulated.
256 devices in a mesh: sec: 32 (over x, y, core), mpo: 8 (over z).
Axes of the slice: x: 4, y: 4, z: 8, core: 2. Of those that a mesh axis runs over, the one named last changes fastest.
Arguments:
- guess: float32 [24576, 256], P('sec'), may hold values from -6 to 6
- left_env: bfloat16 [40, 24576, 768], P('mpo', 'sec'), may hold values from -0.21875 to 0.21875
- right_env: bfloat16 [40, 8192, 256], P('mpo', 'sec'), may hold values from -0.375 to 0.375
- block_rows: int32 [32], replicated, may hold values from 1 to 768, 8192 in all
- charges: int32 [40], P('mpo'), may hold values from -2 to 2, as said below
- ranks: int32 [32], replicated, may hold values from 1 to 256
Outputs:
- wavefunction: float32 [24576, 256], P(('sec', 'mpo'))
- truncated: float32 [24576, 256], P(('sec', 'mpo'))
Inputs may be any that keep to these rules, and one draw needn't show every extreme that they name: The 5 terms of one index of mpo (each aligned run of 5 terms) carry the charges -2, -1, 0, 1, 2 once each.
All inputs are finite; a program needn't handle non-finite values.
Results may differ from a plain program's by a relative error of at most 0.01.
Values may be sent and summed in bfloat16 or wider, within the bound.
No kernel may reach another device: no remote copies, remote signals or barrier semaphores. Data moves between devices by JAX's collectives and lax.ppermute only.
A program may use at most 64 MiB of HBM per device.

v0:
```python
import jax
import jax.numpy as jnp
from jax import lax
from jax.sharding import PartitionSpec as P

MEAN = 256
ITERS = 4


epsilon = 1e-06
step_size = 0.1
highest = lax.Precision.HIGHEST


def sent_to_all(array, axis):
    peers = lax.axis_size(axis)
    return lax.all_to_all(
        jnp.broadcast_to(array[None], (peers, *array.shape)), axis, 0, 0, tiled=True
    )


def of_everyone(array, axis):
    return sent_to_all(array, axis).sum(axis=0)


def passed_along(array, axis, by):
    peers = lax.axis_size(axis)
    return lax.ppermute(array, axis, [(i, (i + by) % peers) for i in range(peers)])


def taken_together(array, axis):
    return sent_to_all(array, axis).astype(jnp.float32).sum(axis=0)


def global_sum(values):
    totals = jax.tree.map(lambda part: of_everyone(part, "sec"), values)
    return totals


def apply_operator(current, left_env, right_env, charges, row_mask):
    rounded = current.astype(jnp.bfloat16)
    shifted = []
    for charge in (-2, -1, 0, 1, 2):
        if charge == 0:
            shifted.append(rounded)
        else:
            shifted.append(passed_along(rounded, "sec", charge))
    stacked = jnp.stack(shifted)
    inputs = jnp.take(stacked, charges + 2, axis=0)
    middle = jnp.einsum(
        "tij,tjk->tik", left_env, inputs, preferred_element_type=jnp.float32
    ).astype(jnp.bfloat16)
    summands = jnp.einsum("tik,tkl->til", middle, right_env, preferred_element_type=jnp.float32)
    applied = taken_together(jnp.sum(summands, axis=0).astype(jnp.bfloat16), "mpo").astype(
        jnp.float32
    )
    return applied * row_mask


def shards(guess, left_env, right_env, block_rows, charges, ranks):
    capacity, right_width = guess.shape
    sectors = block_rows.shape[0]
    sector = lax.axis_index("sec")
    member = lax.axis_index("mpo")
    members = lax.axis_size("mpo")
    slab_rows = capacity // members
    entries = MEAN * sectors * right_width
    sector_ids = jnp.arange(sectors, dtype=jnp.int32)
    own_rows = jnp.sum(jnp.where(sector_ids == sector, block_rows, 0))
    own_rank = jnp.sum(jnp.where(sector_ids == sector, ranks, 0))
    current = guess
    row_mask = (jnp.arange(capacity, dtype=jnp.int32) < own_rows).astype(jnp.float32)[:, None]
    current = current * row_mask
    squares = global_sum((jnp.sum(current * current),))[0]
    current = current * lax.rsqrt(squares / entries + epsilon)
    for repeat in range(ITERS):
        applied = apply_operator(current, left_env, right_env, charges, row_mask)
        self_dot, cross_dot, image_dot = global_sum(
            (jnp.sum(current * current), jnp.sum(current * applied), jnp.sum(applied * applied))
        )
        rayleigh = cross_dot / (self_dot + epsilon)
        update = current - step_size * (applied - rayleigh * current)
        squares = self_dot * (1.0 - (step_size * rayleigh) ** 2) + step_size**2 * image_dot
        current = update * lax.rsqrt(squares / entries + epsilon)
    density = jnp.einsum("ij,ik->jk", current, current, precision=highest)
    slab = lax.dynamic_slice_in_dim(current, member * slab_rows, slab_rows, 0)
    columns = (jnp.arange(right_width, dtype=jnp.int32) < own_rank).astype(jnp.float32)
    span_basis = (jnp.eye(right_width, dtype=jnp.float32) + density / MEAN) * columns[None, :]
    gram_matrix = jnp.einsum("ij,ik->jk", span_basis, span_basis, precision=highest) + jnp.diag(
        1.0 - columns
    )
    factor = jnp.linalg.cholesky(gram_matrix)
    coords = jnp.einsum("ij,jk->ik", slab, span_basis, precision=highest)
    solved = jax.scipy.linalg.cho_solve((factor, True), coords.T).T
    truncated = jnp.einsum("ik,jk->ij", solved, span_basis, precision=highest)
    return (slab, truncated)


def solution(mesh):
    return jax.shard_map(
        shards,
        mesh=mesh,
        in_specs=(P("sec", None), P("mpo", "sec", None), P("mpo", "sec", None), P(), P("mpo"), P()),
        out_specs=(P(("sec", "mpo"), None), P(("sec", "mpo"), None)),
        check_vma=False,
    )
```

profile of v0, /device:TPU:1, one launch (start us, length us, event | category | flops | bytes accessed | tf_op | source)
XLA Modules:
  0.0 681.1 jit_solution(3223830682507111309)
XLA Ops:
  5.4 15.3 %all_to_all.98 = f32[32,1,1]{2,1,0:T(1,128)S(1)} all-to-all(f32[32,1,1]{2,1,0:T(1,128)S(1)} %broadcast_in_dim.65), channel_id=1, replica_groups=mesh['sec'=32,'mpo'=8] {'sec'}, dimensions={0} | all-to-all | bytes 256 | tf_op jit(solution)/shard_map/all_to_all | solution.py:17
  26.8 6.6 collective-permute-done
  33.5 5.3 collective-permute-done.1
  39.1 5.2 collective-permute-done.3
  46.3 5.7 fusion.45
  52.2 80.2 %all_to_all.99 = bf16[8,768,256]{2,1,0:T(8,128)(2,1)S(1)} all-to-all(bf16[8,768,256]{2,1,0:T(8,128)(2,1)S(1)} %broadcast_in_dim.66), channel_id=1, replica_groups=mesh['sec'=32,'mpo'=8] {'mpo'}, dimensions={0} | all-to-all | bytes 6291456 | tf_op jit(solution)/shard_map/all_to_all | solution.py:17
  134.6 8.7 %all_to_all.100 = f32[32,1,1]{2,1,0:T(1,128)S(1)} all-to-all(f32[32,1,1]{2,1,0:T(1,128)S(1)} %broadcast_in_dim.68), channel_id=1, replica_groups=mesh['sec'=32,'mpo'=8] {'sec'}, dimensions={0} | all-to-all | bytes 256 | tf_op jit(solution)/shard_map/all_to_all | solution.py:17
  150.2 5.6 all-to-all-done.2
  163.1 5.0 all-to-all-done.4
  173.3 6.5 collective-permute-done.4
  195.1 5.7 fusion.42
  201.0 74.4 %all_to_all.101 = bf16[8,768,256]{2,1,0:T(8,128)(2,1)S(1)} all-to-all(bf16[8,768,256]{2,1,0:T(8,128)(2,1)S(1)} %broadcast_in_dim.70), channel_id=1, replica_groups=mesh['sec'=32,'mpo'=8] {'mpo'}, dimensions={0} | all-to-all | bytes 6291456 | tf_op jit(solution)/shard_map/all_to_all | solution.py:17
  277.5 9.5 %all_to_all.102 = f32[32,1,1]{2,1,0:T(1,128)S(1)} all-to-all(f32[32,1,1]{2,1,0:T(1,128)S(1)} %broadcast_in_dim.72), channel_id=1, replica_groups=mesh['sec'=32,'mpo'=8] {'sec'}, dimensions={0} | all-to-all | bytes 256 | tf_op jit(solution)/shard_map/all_to_all | solution.py:17
  293.9 5.6 all-to-all-done.6
  306.8 5.0 all-to-all-done.8
  316.7 10.1 %collective-permute-start.11 = (bf16[768,256]{1,0:T(8,128)(2,1)S(1)}, bf16[768,256]{1,0:T(8,128)(2,1)S(1)}, u32[]{:S(2)}, u32[]{:S(2)}) collective-permute-start(bf16[768,256]{1,0:T(8,128)(2,1)S(1)} %get-tuple-element.33), channel_id=1, source_target_pairs={{0,16},{8,24},{16,32},{24,40},{32,48},{40,56},{48,64},{56,72},{64,... | collective-permute-start | bytes 1179656 | tf_op jit(solution)/shard_map/ppermute | solution.py:28
  328.6 12.4 %collective-permute-done.11 = bf16[768,256]{1,0:T(8,128)(2,1)S(1)} collective-permute-done((bf16[768,256]{1,0:T(8,128)(2,1)S(1)}, bf16[768,256]{1,0:T(8,128)(2,1)S(1)}, u32[]{:S(2)}, u32[]{:S(2)}) %collective-permute-start.11) | collective-permute-done | bytes 393248 | tf_op jit(solution)/shard_map/ppermute | solution.py:28
  343.1 5.7 fusion.39
  349.0 76.0 %all_to_all.103 = bf16[8,768,256]{2,1,0:T(8,128)(2,1)S(1)} all-to-all(bf16[8,768,256]{2,1,0:T(8,128)(2,1)S(1)} %broadcast_in_dim.74), channel_id=1, replica_groups=mesh['sec'=32,'mpo'=8] {'mpo'}, dimensions={0} | all-to-all | bytes 6291456 | tf_op jit(solution)/shard_map/all_to_all | solution.py:17
  427.2 10.7 %all_to_all.104 = f32[32,1,1]{2,1,0:T(1,128)S(1)} all-to-all(f32[32,1,1]{2,1,0:T(1,128)S(1)} %broadcast_in_dim.76), channel_id=1, replica_groups=mesh['sec'=32,'mpo'=8] {'sec'}, dimensions={0} | all-to-all | bytes 256 | tf_op jit(solution)/shard_map/all_to_all | solution.py:17
  444.7 5.6 all-to-all-done.10
  457.7 5.0 all-to-all-done.12
  467.6 6.8 collective-permute-done.12
  489.3 5.7 fusion.36
  503.5 70.3 %all-to-all-done.13 = bf16[8,768,256]{2,1,0:T(8,128)(2,1)} async-done(((bf16[8,768,256]{2,1,0:T(8,128)(2,1)}), bf16[8,768,256]{2,1,0:T(8,128)(2,1)}, u32[]{:S(2)}, u32[]{:S(2)}) %all-to-all-start.13) | async-done | bytes 3145760 | tf_op jit(solution)/shard_map/all_to_all | solution.py:17
  582.3 7.0 %all-to-all-done.15 = f32[32,1,1]{2,1,0:T(1,128)S(1)} async-done(((f32[32,1,1]{2,1,0:T(1,128)}), f32[32,1,1]{2,1,0:T(1,128)S(1)}, u32[]{:S(2)}, u32[]{:S(2)}) %all-to-all-start.15) | async-done | bytes 160 | tf_op jit(solution)/shard_map/all_to_all | solution.py:17
  596.1 5.6 all-to-all-done.14
  609.3 4.8 all-to-all-done.16
  617.9 11.7 %cholesky.49 = f32[128,128]{1,0:T(8,128)S(1)} custom-call(f32[128,128]{1,0:T(8,128)S(1)} %cholesky.115), custom_call_target="Cholesky" | custom-call | tf_op jit(solution)/shard_map/jit(cholesky)/cholesky | solution.py:92
  630.0 9.8 %custom-call.18 = f32[1,128,128]{1,2,0:T(8,128)S(1)} custom-call(f32[1,128,128]{2,1,0:T(8,128)S(1)} %get-tuple-element.44), custom_call_target="InvertDiagBlocksLowerTriangular" | custom-call | tf_op jit(solution)/shard_map/jit(cholesky)/cholesky | solution.py:92
  640.3 11.9 %cholesky.103 = f32[128,128]{1,0:T(8,128)S(1)} custom-call(f32[128,128]{1,0:T(8,128)S(1)} %convolution_subtract_fusion), custom_call_target="Cholesky" | custom-call | tf_op jit(solution)/shard_map/jit(cholesky)/cholesky | solution.py:92
  658.6 19.7 %custom-call.19 = f32[2,128,128]{1,2,0:T(8,128)S(1)} custom-call(f32[2,128,128]{2,1,0:T(8,128)S(1)} %get-tuple-element.10), custom_call_target="InvertDiagBlocksLowerTriangular" | custom-call | tf_op jit(solution)/shard_map/jit(_cho_solve)/triangular_solve | solution.py:94
  (151 shorter events, 147.5 us)
Async XLA Ops:
  0.6 45.7 %copy-start = (bf16[5,256,256]{2,1,0:T(8,128)(2,1)S(1)}, bf16[5,256,256]{2,1,0:T(8,128)(2,1)}, u32[]{:S(2)}) copy-start(bf16[5,256,256]{2,1,0:T(8,128)(2,1)} %param.10) | copy-start | bytes 1966084
  0.6 38.2 %copy-start.1 = (f32[768,256]{1,0:T(8,128)S(1)}, f32[768,256]{1,0:T(8,128)}, u32[]{:S(2)}) copy-start(f32[768,256]{1,0:T(8,128)} %param.8) | copy-start | bytes 2359300
  0.7 25.2 %copy-start.3 = (s32[5]{0:T(128)S(1)}, s32[5]{0:T(128)}, u32[]{:S(2)}) copy-start(s32[5]{0:T(128)} %param.12) | copy-start | bytes 64
  23.4 10.1 %collective-permute-start = (bf16[768,256]{1,0:T(8,128)(2,1)S(1)}, bf16[768,256]{1,0:T(8,128)(2,1)S(1)}, u32[]{:S(2)}, u32[]{:S(2)}) collective-permute-start(bf16[768,256]{1,0:T(8,128)(2,1)S(1)} %fusion.74), channel_id=1, source_target_pairs={{0,240},{8,248},{16,0},{24,8},{32,16},{40,24},{48,32},{56,40},{64,... | collective-permute-start | bytes 1179656 | tf_op jit(solution)/shard_map/ppermute | solution.py:28
  25.0 13.8 %collective-permute-start.1 = (bf16[768,256]{1,0:T(8,128)(2,1)S(1)}, bf16[768,256]{1,0:T(8,128)(2,1)S(1)}, u32[]{:S(2)}, u32[]{:S(2)}) collective-permute-start(bf16[768,256]{1,0:T(8,128)(2,1)S(1)} %fusion.74), channel_id=1, source_target_pairs={{0,248},{8,0},{16,8},{24,16},{32,24},{40,32},{48,40},{56,48},{64,5... | collective-permute-start | bytes 1179656 | tf_op jit(solution)/shard_map/ppermute | solution.py:28
  25.9 13.1 %collective-permute-start.2 = (bf16[768,256]{1,0:T(8,128)(2,1)S(1)}, bf16[768,256]{1,0:T(8,128)(2,1)S(1)}, u32[]{:S(2)}, u32[]{:S(2)}) collective-permute-start(bf16[768,256]{1,0:T(8,128)(2,1)S(1)} %fusion.74), channel_id=1, source_target_pairs={{0,8},{8,16},{16,24},{24,32},{32,40},{40,48},{48,56},{56,64},{64,7... | collective-permute-start | bytes 1179656 | tf_op jit(solution)/shard_map/ppermute | solution.py:28
  26.8 17.4 %collective-permute-start.3 = (bf16[768,256]{1,0:T(8,128)(2,1)S(1)}, bf16[768,256]{1,0:T(8,128)(2,1)S(1)}, u32[]{:S(2)}, u32[]{:S(2)}) collective-permute-start(bf16[768,256]{1,0:T(8,128)(2,1)S(1)} %fusion.74), channel_id=1, source_target_pairs={{0,16},{8,24},{16,32},{24,40},{32,48},{40,56},{48,64},{56,72},{64,... | collective-permute-start | bytes 1179656 | tf_op jit(solution)/shard_map/ppermute | solution.py:28
  144.6 11.1 %all-to-all-start.2 = ((f32[32,1,1]{2,1,0:T(1,128)}), f32[32,1,1]{2,1,0:T(1,128)S(1)}, u32[]{:S(2)}, u32[]{:S(2)}) async-start(f32[32,1,1]{2,1,0:T(1,128)} %broadcast_in_dim.67), calls=%async_computation.2 | async-start | bytes 32768 | tf_op jit(solution)/shard_map/all_to_all | solution.py:17
  157.0 11.1 %all-to-all-start.4 = ((f32[32,1,1]{2,1,0:T(1,128)}), f32[32,1,1]{2,1,0:T(1,128)S(1)}, u32[]{:S(2)}, u32[]{:S(2)}) async-start(f32[32,1,1]{2,1,0:T(1,128)} %broadcast_in_dim.69), calls=%async_computation.4 | async-start | bytes 32768 | tf_op jit(solution)/shard_map/all_to_all | solution.py:17
  169.7 10.1 %collective-permute-start.4 = (bf16[768,256]{1,0:T(8,128)(2,1)S(1)}, bf16[768,256]{1,0:T(8,128)(2,1)S(1)}, u32[]{:S(2)}, u32[]{:S(2)}) collective-permute-start(bf16[768,256]{1,0:T(8,128)(2,1)S(1)} %get-tuple-element.35), channel_id=1, source_target_pairs={{0,240},{8,248},{16,0},{24,8},{32,16},{40,24},{48,32},{56,40},{64,... | collective-permute-start | bytes 1179656 | tf_op jit(solution)/shard_map/ppermute | solution.py:28
  171.3 13.9 %collective-permute-start.5 = (bf16[768,256]{1,0:T(8,128)(2,1)S(1)}, bf16[768,256]{1,0:T(8,128)(2,1)S(1)}, u32[]{:S(2)}, u32[]{:S(2)}) collective-permute-start(bf16[768,256]{1,0:T(8,128)(2,1)S(1)} %get-tuple-element.35), channel_id=1, source_target_pairs={{0,248},{8,0},{16,8},{24,16},{32,24},{40,32},{48,40},{56,48},{64,5... | collective-permute-start | bytes 1179656 | tf_op jit(solution)/shard_map/ppermute | solution.py:28
  172.2 14.5 %collective-permute-start.6 = (bf16[768,256]{1,0:T(8,128)(2,1)S(1)}, bf16[768,256]{1,0:T(8,128)(2,1)S(1)}, u32[]{:S(2)}, u32[]{:S(2)}) collective-permute-start(bf16[768,256]{1,0:T(8,128)(2,1)S(1)} %get-tuple-element.35), channel_id=1, source_target_pairs={{0,8},{8,16},{16,24},{24,32},{32,40},{40,48},{48,56},{56,64},{64,7... | collective-permute-start | bytes 1179656 | tf_op jit(solution)/shard_map/ppermute | solution.py:28
  173.2 17.4 %collective-permute-start.7 = (bf16[768,256]{1,0:T(8,128)(2,1)S(1)}, bf16[768,256]{1,0:T(8,128)(2,1)S(1)}, u32[]{:S(2)}, u32[]{:S(2)}) collective-permute-start(bf16[768,256]{1,0:T(8,128)(2,1)S(1)} %get-tuple-element.35), channel_id=1, source_target_pairs={{0,16},{8,24},{16,32},{24,40},{32,48},{40,56},{48,64},{56,72},{64,... | collective-permute-start | bytes 1179656 | tf_op jit(solution)/shard_map/ppermute | solution.py:28
  288.3 11.1 %all-to-all-start.6 = ((f32[32,1,1]{2,1,0:T(1,128)}), f32[32,1,1]{2,1,0:T(1,128)S(1)}, u32[]{:S(2)}, u32[]{:S(2)}) async-start(f32[32,1,1]{2,1,0:T(1,128)} %broadcast_in_dim.71), calls=%async_computation.6 | async-start | bytes 32768 | tf_op jit(solution)/shard_map/all_to_all | solution.py:17
  300.7 11.1 %all-to-all-start.8 = ((f32[32,1,1]{2,1,0:T(1,128)}), f32[32,1,1]{2,1,0:T(1,128)S(1)}, u32[]{:S(2)}, u32[]{:S(2)}) async-start(f32[32,1,1]{2,1,0:T(1,128)} %broadcast_in_dim.73), calls=%async_computation.8 | async-start | bytes 32768 | tf_op jit(solution)/shard_map/all_to_all | solution.py:17
  313.4 13.4 %collective-permute-start.8 = (bf16[768,256]{1,0:T(8,128)(2,1)S(1)}, bf16[768,256]{1,0:T(8,128)(2,1)S(1)}, u32[]{:S(2)}, u32[]{:S(2)}) collective-permute-start(bf16[768,256]{1,0:T(8,128)(2,1)S(1)} %get-tuple-element.33), channel_id=1, source_target_pairs={{0,240},{8,248},{16,0},{24,8},{32,16},{40,24},{48,32},{56,40},{64,... | collective-permute-start | bytes 1179656 | tf_op jit(solution)/shard_map/ppermute | solution.py:28
  314.9 13.6 %collective-permute-start.9 = (bf16[768,256]{1,0:T(8,128)(2,1)S(1)}, bf16[768,256]{1,0:T(8,128)(2,1)S(1)}, u32[]{:S(2)}, u32[]{:S(2)}) collective-permute-start(bf16[768,256]{1,0:T(8,128)(2,1)S(1)} %get-tuple-element.33), channel_id=1, source_target_pairs={{0,248},{8,0},{16,8},{24,16},{32,24},{40,32},{48,40},{56,48},{64,5... | collective-permute-start | bytes 1179656 | tf_op jit(solution)/shard_map/ppermute | solution.py:28
  315.8 12.8 %collective-permute-start.10 = (bf16[768,256]{1,0:T(8,128)(2,1)S(1)}, bf16[768,256]{1,0:T(8,128)(2,1)S(1)}, u32[]{:S(2)}, u32[]{:S(2)}) collective-permute-start(bf16[768,256]{1,0:T(8,128)(2,1)S(1)} %get-tuple-element.33), channel_id=1, source_target_pairs={{0,8},{8,16},{16,24},{24,32},{32,40},{40,48},{48,56},{56,64},{64,7... | collective-permute-start | bytes 1179656 | tf_op jit(solution)/shard_map/ppermute | solution.py:28
  316.7 24.4 %collective-permute-start.11 = (bf16[768,256]{1,0:T(8,128)(2,1)S(1)}, bf16[768,256]{1,0:T(8,128)(2,1)S(1)}, u32[]{:S(2)}, u32[]{:S(2)}) collective-permute-start(bf16[768,256]{1,0:T(8,128)(2,1)S(1)} %get-tuple-element.33), channel_id=1, source_target_pairs={{0,16},{8,24},{16,32},{24,40},{32,48},{40,56},{48,64},{56,72},{64,... | collective-permute-start | bytes 1179656 | tf_op jit(solution)/shard_map/ppermute | solution.py:28
  439.2 11.1 %all-to-all-start.10 = ((f32[32,1,1]{2,1,0:T(1,128)}), f32[32,1,1]{2,1,0:T(1,128)S(1)}, u32[]{:S(2)}, u32[]{:S(2)}) async-start(f32[32,1,1]{2,1,0:T(1,128)} %broadcast_in_dim.75), calls=%async_computation.10 | async-start | bytes 32768 | tf_op jit(solution)/shard_map/all_to_all | solution.py:17
  451.6 11.1 %all-to-all-start.12 = ((f32[32,1,1]{2,1,0:T(1,128)}), f32[32,1,1]{2,1,0:T(1,128)S(1)}, u32[]{:S(2)}, u32[]{:S(2)}) async-start(f32[32,1,1]{2,1,0:T(1,128)} %broadcast_in_dim.77), calls=%async_computation.12 | async-start | bytes 32768 | tf_op jit(solution)/shard_map/all_to_all | solution.py:17
  464.2 10.1 %collective-permute-start.12 = (bf16[768,256]{1,0:T(8,128)(2,1)S(1)}, bf16[768,256]{1,0:T(8,128)(2,1)S(1)}, u32[]{:S(2)}, u32[]{:S(2)}) collective-permute-start(bf16[768,256]{1,0:T(8,128)(2,1)S(1)} %get-tuple-element.31), channel_id=1, source_target_pairs={{0,240},{8,248},{16,0},{24,8},{32,16},{40,24},{48,32},{56,40},{64,... | collective-permute-start | bytes 1179656 | tf_op jit(solution)/shard_map/ppermute | solution.py:28
  465.8 13.9 %collective-permute-start.13 = (bf16[768,256]{1,0:T(8,128)(2,1)S(1)}, bf16[768,256]{1,0:T(8,128)(2,1)S(1)}, u32[]{:S(2)}, u32[]{:S(2)}) collective-permute-start(bf16[768,256]{1,0:T(8,128)(2,1)S(1)} %get-tuple-element.31), channel_id=1, source_target_pairs={{0,248},{8,0},{16,8},{24,16},{32,24},{40,32},{48,40},{56,48},{64,5... | collective-permute-start | bytes 1179656 | tf_op jit(solution)/shard_map/ppermute | solution.py:28
  466.7 14.5 %collective-permute-start.14 = (bf16[768,256]{1,0:T(8,128)(2,1)S(1)}, bf16[768,256]{1,0:T(8,128)(2,1)S(1)}, u32[]{:S(2)}, u32[]{:S(2)}) collective-permute-start(bf16[768,256]{1,0:T(8,128)(2,1)S(1)} %get-tuple-element.31), channel_id=1, source_target_pairs={{0,8},{8,16},{16,24},{24,32},{32,40},{40,48},{48,56},{56,64},{64,7... | collective-permute-start | bytes 1179656 | tf_op jit(solution)/shard_map/ppermute | solution.py:28
  467.5 17.4 %collective-permute-start.15 = (bf16[768,256]{1,0:T(8,128)(2,1)S(1)}, bf16[768,256]{1,0:T(8,128)(2,1)S(1)}, u32[]{:S(2)}, u32[]{:S(2)}) collective-permute-start(bf16[768,256]{1,0:T(8,128)(2,1)S(1)} %get-tuple-element.31), channel_id=1, source_target_pairs={{0,16},{8,24},{16,32},{24,40},{32,48},{40,56},{48,64},{56,72},{64,... | collective-permute-start | bytes 1179656 | tf_op jit(solution)/shard_map/ppermute | solution.py:28
  496.9 4.6 copy-start.4
  496.9 76.8 %all-to-all-start.13 = ((bf16[8,768,256]{2,1,0:T(8,128)(2,1)}), bf16[8,768,256]{2,1,0:T(8,128)(2,1)}, u32[]{:S(2)}, u32[]{:S(2)}) async-start(bf16[8,768,256]{2,1,0:T(8,128)(2,1)} %broadcast_in_dim.78), calls=%async_computation.13 | async-start | bytes 6291456 | tf_op jit(solution)/shard_map/all_to_all | solution.py:17
  578.3 11.0 %all-to-all-start.15 = ((f32[32,1,1]{2,1,0:T(1,128)}), f32[32,1,1]{2,1,0:T(1,128)S(1)}, u32[]{:S(2)}, u32[]{:S(2)}) async-start(f32[32,1,1]{2,1,0:T(1,128)} %broadcast_in_dim.80), calls=%async_computation.15 | async-start | bytes 32768 | tf_op jit(solution)/shard_map/all_to_all | solution.py:17
  590.5 11.1 %all-to-all-start.14 = ((f32[32,1,1]{2,1,0:T(1,128)}), f32[32,1,1]{2,1,0:T(1,128)S(1)}, u32[]{:S(2)}, u32[]{:S(2)}) async-start(f32[32,1,1]{2,1,0:T(1,128)} %broadcast_in_dim.79), calls=%async_computation.14 | async-start | bytes 32768 | tf_op jit(solution)/shard_map/all_to_all | solution.py:17
  602.9 11.1 %all-to-all-start.16 = ((f32[32,1,1]{2,1,0:T(1,128)}), f32[32,1,1]{2,1,0:T(1,128)S(1)}, u32[]{:S(2)}, u32[]{:S(2)}) async-start(f32[32,1,1]{2,1,0:T(1,128)} %broadcast_in_dim.81), calls=%async_computation.16 | async-start | bytes 32768 | tf_op jit(solution)/shard_map/all_to_all | solution.py:17
  629.7 51.0 %copy-start.2 = (f32[96,256]{1,0:T(8,128)}, f32[96,256]{1,0:T(8,128)S(1)}, u32[]{:S(2)}) copy-start(f32[96,256]{1,0:T(8,128)S(1)} %constant_dynamic-slice_fusion.1) | copy-start | bytes 294916
where the time goes:
time: 691 us; the launch traced here: 681 us
  blocking collectives  275 us (40%)
  waiting for transfers between devices  179 us (26%)
  other arithmetic  78.8 us (11%)
  starting transfers between devices  65.5 us (9%)
  local copies, waits for them, and re-layouts  40.2 us (6%)
  matrix products  27.9 us (4%)
  between operations  14.7 us (2%)
    all_to_all x7, blocking collectives, sent_to_all(): lax.all_to_all(jnp.broadcast_to(array[None], (peers, *array.shape)), axis...  275 us
    all_to_all x10, waiting for transfers between devices, sent_to_all(): lax.all_to_all(jnp.broadcast_to(array[None], (peers, *array.shape)), axis...  119 us
    ppermute x16, waiting for transfers between devices, passed_along(): lax.ppermute(array, axis, [(i, (i + by) % peers) for i in range(peers)])  59.8 us
    all_to_all x10, starting transfers between devices, sent_to_all(): lax.all_to_all(jnp.broadcast_to(array[None], (peers, *array.shape)), axis...  41.9 us
    another operation x6, other arithmetic, shards(): factor = jnp.linalg.cholesky(gram_matrix)  34.3 us
    ppermute x16, starting transfers between devices, passed_along(): lax.ppermute(array, axis, [(i, (i + by) % peers) for i in range(peers)])  23.6 us
    dot_general x4, matrix products, apply_operator(): jnp.einsum('tik,tkl->til', middle, right_env, preferred_element_type=jnp....  22.7 us
    another operation x3, other arithmetic, shards(): solved = jax.scipy.linalg.cho_solve((factor, True), coords.T).T  19.7 us
  transfers between devices with their start and end apart: 26, of which 21 were waited for; matrix products, arithmetic and copies ran while one was open for 2% of the time, Pallas kernels for 0%

commit v1 on v0

v1 whole, which is shorter than its diff:
```python
import jax
import jax.numpy as jnp
from jax import lax
from jax.experimental import pallas as pl
from jax.experimental.pallas import tpu as pltpu
from jax.sharding import PartitionSpec as P

MEAN = 256
ITERS = 4
REACH = 2
SHRINK = 2.0**-7
epsilon = 1e-06
step_size = 0.1
highest = lax.Precision.HIGHEST
TILE = 256
BASE = 64


def sent_to_all(array, axis):
    peers = lax.axis_size(axis)
    return lax.all_to_all(
        jnp.broadcast_to(array[None], (peers, *array.shape)), axis, 0, 0, tiled=True
    )


def passed_along(array, axis, by):
    peers = lax.axis_size(axis)
    return lax.ppermute(array, axis, [(i, (i + by) % peers) for i in range(peers)])


def operator_body(rows_ref, charges_ref, *refs):
    blocks = refs[: 2 * REACH + 1]
    left_ref, right_ref, out_ref, held, total, sems = refs[2 * REACH + 1 :]
    term = pl.program_id(0)
    copies = [
        pltpu.make_async_copy(block, held.at[i], sems.at[i]) for i, block in enumerate(blocks)
    ]

    @pl.when(term == 0)
    def _():
        for copy in copies:
            copy.start()
        total[...] = jnp.zeros_like(total)
        for copy in copies:
            copy.wait()

    shift = charges_ref[term]
    own_rows = rows_ref[REACH]
    source_rows = rows_ref[REACH - shift]
    slot = REACH + shift
    tiles = held.shape[1] // TILE
    for i in range(tiles):
        for j in range(1, tiles + 1):
            low, high = (j - 1) * TILE, j * TILE
            fits = (own_rows > i * TILE) & (source_rows > low)
            if j < tiles:
                fits = fits & (source_rows <= high)

            @pl.when(fits)
            def _():
                span = pl.ds(i * TILE, TILE)
                middle = jnp.dot(
                    left_ref[0, span, :high],
                    held[slot, :high, :],
                    preferred_element_type=jnp.float32,
                ).astype(jnp.bfloat16)
                total[span, :] += jnp.dot(
                    middle, right_ref[0], preferred_element_type=jnp.float32
                )

    @pl.when(term == pl.num_programs(0) - 1)
    def _():
        row = lax.broadcasted_iota(jnp.int32, total.shape, 0)
        out_ref[...] = jnp.where(row < own_rows, total[...] * SHRINK, 0.0).astype(out_ref.dtype)


def apply_terms(rows, charges, blocks, left_env, right_env):
    terms, capacity, _ = left_env.shape
    width = right_env.shape[-1]
    count = len(blocks)
    return pl.pallas_call(
        operator_body,
        grid_spec=pltpu.PrefetchScalarGridSpec(
            num_scalar_prefetch=2,
            grid=(terms,),
            in_specs=[pl.BlockSpec(memory_space=pl.ANY)] * count
            + [
                pl.BlockSpec((1, capacity, capacity), lambda w, *_: (w, 0, 0)),
                pl.BlockSpec((1, width, width), lambda w, *_: (w, 0, 0)),
            ],
            out_specs=pl.BlockSpec((capacity, width), lambda w, *_: (0, 0)),
            scratch_shapes=[
                pltpu.VMEM((count, capacity, width), jnp.bfloat16),
                pltpu.VMEM((capacity, width), jnp.float32),
                pltpu.SemaphoreType.DMA((count,)),
            ],
        ),
        out_shape=jax.ShapeDtypeStruct((capacity, width), jnp.bfloat16),
        compiler_params=pltpu.CompilerParams(vmem_limit_bytes=40 << 20),
        name="apply_terms",
    )(rows, charges, *blocks, left_env, right_env)


PAIRS = [(i, j) for i in range(ITERS + 1) for j in range(i, ITERS + 1)]


def products_body(rows_ref, first_ref, *refs):
    powers, out_ref = refs[:-1], refs[-1]
    arrays = [first_ref[...]] + [ref[...].astype(jnp.float32) for ref in powers]
    lane = lax.broadcasted_iota(jnp.int32, (1, 128), 1)
    out = jnp.zeros((1, 128), jnp.float32)
    for place, (i, j) in enumerate(PAIRS):
        value = jnp.sum(jnp.sum(arrays[i] * arrays[j], axis=0, keepdims=True), axis=1, keepdims=True)
        out = out + jnp.where(lane == place, value, 0.0)
    out_ref[...] = out


def products(start, powers):
    return pl.pallas_call(
        lambda *refs: products_body(None, *refs),
        out_shape=jax.ShapeDtypeStruct((1, 128), jnp.float32),
        compiler_params=pltpu.CompilerParams(vmem_limit_bytes=40 << 20),
        name="products",
    )(start, *powers)


def dot32(a, b, dims):
    return lax.dot_general(
        a, b, (dims, ((), ())), precision=highest, preferred_element_type=jnp.float32
    )


def swept_block(block):
    size = block.shape[0]
    row = lax.broadcasted_iota(jnp.int32, block.shape, 0)
    lane = lax.broadcasted_iota(jnp.int32, block.shape, 1)
    for k in range(size):
        pivot_row = block[k : k + 1, :]
        pivot_col = block[:, k : k + 1]
        inverse = 1.0 / block[k : k + 1, k : k + 1]
        scaled = pivot_row * inverse
        update = block - pivot_col * scaled
        update = jnp.where(lane == k, pivot_col * inverse, update)
        update = jnp.where(row == k, scaled, update)
        block = jnp.where((row == k) & (lane == k), -inverse, update)
    return -block


def tail_body(info_ref, sums_ref, start_ref, *refs):
    powers = refs[:ITERS]
    slab_ref, cut_ref, state, gram = refs[ITERS:]
    entries = info_ref[2].astype(jnp.float32)
    summed = jnp.sum(sums_ref[...], axis=0, keepdims=True)
    table = {}
    for place, (i, j) in enumerate(PAIRS):
        table[i, j] = table[j, i] = summed[:, place : place + 1]

    def inner(a, b):
        out = 0.0
        for i, x in enumerate(a):
            for j, y in enumerate(b):
                if x is not None and y is not None:
                    out = out + x * y * table[i, j]
        return out

    def scale_of(squares):
        return lax.rsqrt(squares / entries + epsilon)

    weights = [scale_of(table[0, 0])] + [None] * ITERS
    for _ in range(ITERS):
        image = [None] + [None if x is None else x * (1.0 / SHRINK) for x in weights[:-1]]
        rayleigh = inner(weights, image) / (inner(weights, weights) + epsilon)
        update = []
        for x, y in zip(weights, image):
            value = None
            if x is not None:
                value = x * (1.0 + step_size * rayleigh)
            if y is not None:
                value = -step_size * y if value is None else value - step_size * y
            update.append(value)
        scale = scale_of(jnp.maximum(inner(update, update), 0.0))
        weights = [None if x is None else x * scale for x in update]

    current = weights[0] * start_ref[...]
    for weight, ref in zip(weights[1:], powers):
        current = current + weight * ref[...].astype(jnp.float32)
    state[...] = current
    density = dot32(current, current, ((0,), (0,)))
    width = density.shape[0]
    row = lax.broadcasted_iota(jnp.int32, density.shape, 0)
    lane = lax.broadcasted_iota(jnp.int32, density.shape, 1)
    diagonal = (row == lane).astype(jnp.float32)
    kept = lane < info_ref[1]
    basis = jnp.where(kept, diagonal + density * (1.0 / MEAN), 0.0)
    gram[...] = dot32(basis, basis, ((0,), (0,))) + jnp.where(kept, 0.0, diagonal)
    panel_row = lax.broadcasted_iota(jnp.int32, (BASE, width), 0)
    panel_lane = lax.broadcasted_iota(jnp.int32, (BASE, width), 1)
    for b in range(width // BASE):
        low = b * BASE
        panel = gram[low : low + BASE, :]
        inverse = swept_block(panel[:, low : low + BASE])
        inside = (panel_lane >= low) & (panel_lane < low + BASE)
        select = (panel_lane == panel_row + low).astype(jnp.float32)
        rest = jnp.where(inside, 0.0, panel)
        solved = dot32(inverse, rest, ((1,), (0,)))
        change = dot32(
            jnp.concatenate([rest, solved], axis=0),
            jnp.concatenate([solved, -select], axis=0),
            ((0,), (0,)),
        )
        held = (lane >= low) & (lane < low + BASE)
        gram[...] = jnp.where(held, 0.0, gram[...]) - change
        gram[low : low + BASE, :] = solved - dot32(inverse, select, ((1,), (0,)))
    slab_rows = slab_ref.shape[0]
    slab = state[pl.ds(pl.multiple_of(info_ref[0] * slab_rows, 8), slab_rows), :]
    slab_ref[...] = slab
    coords = dot32(slab, basis, ((1,), (0,)))
    solved = -dot32(coords, gram[...], ((1,), (0,)))
    cut_ref[...] = dot32(solved, basis, ((1,), (1,)))


def tail(info, sums, start, powers, slab_rows):
    capacity, width = start.shape
    vmem = pl.BlockSpec(memory_space=pltpu.VMEM)
    return pl.pallas_call(
        tail_body,
        in_specs=[pl.BlockSpec(memory_space=pltpu.SMEM)] + [vmem] * (2 + ITERS),
        out_shape=[jax.ShapeDtypeStruct((slab_rows, width), jnp.float32)] * 2,
        scratch_shapes=[
            pltpu.VMEM((capacity, width), jnp.float32),
            pltpu.VMEM((width, width), jnp.float32),
        ],
        compiler_params=pltpu.CompilerParams(vmem_limit_bytes=40 << 20),
        name="truncate",
    )(info, sums, start, *powers)


def shards(guess, left_env, right_env, block_rows, charges, ranks):
    capacity, width = guess.shape
    sectors = block_rows.shape[0]
    sector = lax.axis_index("sec")
    member = lax.axis_index("mpo")
    members = lax.axis_size("mpo")
    slab_rows = capacity // members
    rows = jnp.stack([block_rows[(sector + d) % sectors] for d in range(-REACH, REACH + 1)])
    own_rows = rows[REACH]
    start = jnp.where(jnp.arange(capacity, dtype=jnp.int32)[:, None] < own_rows, guess, 0.0)
    whole = start.astype(jnp.bfloat16)
    powers = []
    for repeat in range(ITERS):
        blocks = [
            whole if by == 0 else passed_along(whole, "sec", by)
            for by in range(-REACH, REACH + 1)
        ]
        part = apply_terms(rows, charges, blocks, left_env, right_env)
        pieces = lax.all_to_all(
            part.reshape(members, slab_rows, width), "mpo", 0, 0, tiled=True
        )
        slab = jnp.sum(pieces.astype(jnp.float32), axis=0).astype(jnp.bfloat16)
        whole = sent_to_all(slab, "mpo").reshape(capacity, width)
        powers.append(whole)
    sums = sent_to_all(products(start, powers), "sec").reshape(sectors, 128)
    info = jnp.stack([member, ranks[sector], MEAN * sectors * width]).astype(jnp.int32)
    slab, cut = tail(info, sums, start, powers, slab_rows)
    return (slab, cut)


def solution(mesh):
    return jax.shard_map(
        shards,
        mesh=mesh,
        in_specs=(P("sec", None), P("mpo", "sec", None), P("mpo", "sec", None), P(), P("mpo"), P()),
        out_specs=(P(("sec", "mpo"), None), P(("sec", "mpo"), None)),
        check_vma=False,
    )
```

time: 691 us -> 311 us (0.45)
  blocking collectives: 275 us -> 97.1 us
  waiting for transfers between devices: 179 us -> 41.6 us
  other arithmetic: 78.8 us -> 2.88 us
  Pallas kernels: 0 us -> 56.1 us
  matrix products: 27.9 us -> 0 us
  starting transfers between devices: 65.5 us -> 86.9 us
  local copies, waits for them, and re-layouts: 40.2 us -> 19.3 us
  between operations: 14.7 us -> 1.07 us
    all_to_all x7 -> x3, blocking collectives: 275 us -> 39.7 us  [sent_to_all(): lax.all_to_all(jnp.broadcast_to(array[None], (peers, *array.shape)), axis...]
    all_to_all x10 -> x2, waiting for transfers between devices: 119 us -> 10.1 us  [sent_to_all(): lax.all_to_all(jnp.broadcast_to(array[None], (peers, *array.shape)), axis...]
    all_to_all x0 -> x4, blocking collectives: none -> 57.4 us  [shards(): lax.all_to_all(part.reshape(members, slab_rows, width), 'mpo', 0, 0, tile...]
    pallas_call x0 -> x6, Pallas kernels: none -> 56.1 us  [the longest x1 40 us: tail(): pl.pallas_call(tail_body, in_specs=[pl.BlockSpec(memory_space=pltpu.SMEM)...]
    another operation x9 -> x1, other arithmetic: 54 us -> 0.72 us  [shards(): jnp.stack([member, ranks[sector], MEAN * sectors * width]).astype(jnp.int32)]
    ppermute x16, starting transfers between devices: 23.6 us -> 56.6 us  [passed_along(): lax.ppermute(array, axis, [(i, (i + by) % peers) for i in range(peers)])]
    ppermute x16, waiting for transfers between devices: 59.8 us -> 31.5 us  [passed_along(): lax.ppermute(array, axis, [(i, (i + by) % peers) for i in range(peers)])]
    dot_general x8 -> x0, matrix products: 26.1 us -> none  [the longest x4 22.7 us: apply_operator(): jnp.einsum('tik,tkl->til', middle, right_env, preferred_element_type=jnp....]
  transfers between devices with their start and end apart: 26 -> 18, of which waited for: 21 -> 14; matrix products, arithmetic and copies ran while one was open for 2% -> 1% of each run, Pallas kernels for 0% -> 0%
where the time goes in v1:
time: 311 us; the launch traced here: 305 us
  blocking collectives  97.1 us (31%)
  starting transfers between devices  86.9 us (28%)
  Pallas kernels  56.1 us (18%)
  waiting for transfers between devices  41.6 us (13%)
  local copies, waits for them, and re-layouts  19.3 us (6%)
    all_to_all x4, blocking collectives, shards(): lax.all_to_all(part.reshape(members, slab_rows, width), 'mpo', 0, 0, tile...  57.4 us
    ppermute x16, starting transfers between devices, passed_along(): lax.ppermute(array, axis, [(i, (i + by) % peers) for i in range(peers)])  56.6 us
    pallas_call x1, Pallas kernels, tail(): pl.pallas_call(tail_body, in_specs=[pl.BlockSpec(memory_space=pltpu.SMEM)...  40 us
    all_to_all x3, blocking collectives, sent_to_all(): lax.all_to_all(jnp.broadcast_to(array[None], (peers, *array.shape)), axis...  39.7 us
    ppermute x16, waiting for transfers between devices, passed_along(): lax.ppermute(array, axis, [(i, (i + by) % peers) for i in range(peers)])  31.5 us
    all_to_all x2, starting transfers between devices, sent_to_all(): lax.all_to_all(jnp.broadcast_to(array[None], (peers, *array.shape)), axis...  30.3 us
    pallas_call x4, Pallas kernels, apply_terms(): pl.pallas_call(operator_body, grid_spec=pltpu.PrefetchScalarGridSpec(num_...  15.4 us
    unnamed x18, local copies, waits for them, and re-layouts  12.4 us
  transfers between devices with their start and end apart: 18, of which 14 were waited for; matrix products, arithmetic and copies ran while one was open for 1% of the time, Pallas kernels for 0%

profile of v1, /device:TPU:1, one launch (start us, length us, event | category | flops | bytes accessed | tf_op | source)
XLA Modules:
  0.0 304.9 jit_solution(654796584768305734)
XLA Ops:
  4.2 2.2 collective-permute-start.3
  8.6 4.0 %collective-permute-start = (bf16[768,256]{1,0:T(8,128)(2,1)S(1)}, bf16[768,256]{1,0:T(8,128)(2,1)S(1)}, u32[]{:S(2)}, u32[]{:S(2)}) collective-permute-start(bf16[768,256]{1,0:T(8,128)(2,1)S(1)} %get-tuple-element.2.refs_2_), channel_id=1, source_target_pairs={{0,240},{8,248},{16,0},{24,8},{32,16},{40,24},{48,32},{56,40},{64,... | collective-permute-start | bytes 1179656 | tf_op jit(solution)/shard_map/ppermute | solution.py:28
  12.6 3.2 %stack.11.rows_ref = s32[5]{0:T(128)S(1)} concatenate(s32[1]{0:T(128)} %get-tuple-element.6, s32[1]{0:T(128)} %get-tuple-element.5, s32[1]{0:T(128)} %get-tuple-element.7, s32[1]{0:T(128)} %get-tuple-element.8, s32[1]{0:T(128)} %get-tuple-element.4), dimensions={0} | concatenate | bytes 40 | tf_op jit(solution)/shard_map/stack | solution.py:245
  16.9 2.6 collective-permute-done.2.refs_3_
  21.3 2.7 copy-done
  25.7 3.9 %apply_terms.4 = bf16[768,256]{1,0:T(8,128)(2,1)S(1)} custom-call(s32[5]{0:T(128)S(1)} %stack.11.rows_ref, s32[5]{0:T(128)S(1)} %copy-done.6, bf16[768,256]{1,0:T(8,128)(2,1)S(1)} %collective-permute-done.refs_0_, bf16[768,256]{1,0:T(8,128)(2,1)S(1)} %collective-permute-done.1.refs_1_, bf16[768,256]{1,0:T(8,128)(2,1)S(1)} %get-tuple-element.2.refs_2_, ...), custom_call_target="tpu_custom_call" | custom-call | tf_op jit(solution)/shard_map/apply_terms/pallas_call | solution.py:81
  29.6 18.0 %all_to_all.45 = bf16[8,96,256]{2,1,0:T(8,128)(2,1)S(1)} all-to-all(bf16[8,96,256]{2,1,0:T(8,128)(2,1)S(1)} %bitcast.35), channel_id=1, replica_groups=mesh['sec'=32,'mpo'=8] {'mpo'}, dimensions={0} | all-to-all | bytes 786432 | tf_op jit(solution)/shard_map/all_to_all | solution.py:256
  47.6 13.5 %all_to_all.46 = bf16[8,96,256]{2,1,0:T(8,128)(2,1)S(1)} all-to-all(bf16[8,96,256]{2,1,0:T(8,128)(2,1)S(1)} %broadcast_in_dim.26), channel_id=1, replica_groups=mesh['sec'=32,'mpo'=8] {'mpo'}, dimensions={0} | all-to-all | bytes 786432 | tf_op jit(solution)/shard_map/all_to_all | solution.py:21
  61.3 9.6 %collective-permute-start.6 = (bf16[768,256]{1,0:T(8,128)(2,1)S(1)}, bf16[768,256]{1,0:T(8,128)(2,1)S(1)}, u32[]{:S(2)}, u32[]{:S(2)}) collective-permute-start(bf16[768,256]{1,0:T(8,128)(2,1)S(1)} %bitcast.13), channel_id=1, source_target_pairs={{0,8},{8,16},{16,24},{24,32},{32,40},{40,48},{48,56},{56,64},{64,7... | collective-permute-start | bytes 1179656 | tf_op jit(solution)/shard_map/ppermute | solution.py:28
  72.4 5.1 %collective-permute-start.4 = (bf16[768,256]{1,0:T(8,128)(2,1)S(1)}, bf16[768,256]{1,0:T(8,128)(2,1)S(1)}, u32[]{:S(2)}, u32[]{:S(2)}) collective-permute-start(bf16[768,256]{1,0:T(8,128)(2,1)S(1)} %bitcast.15), channel_id=1, source_target_pairs={{0,240},{8,248},{16,0},{24,8},{32,16},{40,24},{48,32},{56,40},{64,... | collective-permute-start | bytes 1179656 | tf_op jit(solution)/shard_map/ppermute | solution.py:28
  79.6 6.7 %collective-permute-done.4.refs_0_ = bf16[768,256]{1,0:T(8,128)(2,1)S(1)} collective-permute-done((bf16[768,256]{1,0:T(8,128)(2,1)S(1)}, bf16[768,256]{1,0:T(8,128)(2,1)S(1)}, u32[]{:S(2)}, u32[]{:S(2)}) %collective-permute-start.4) | collective-permute-done | bytes 393248 | tf_op jit(solution)/shard_map/ppermute | solution.py:28
  86.2 2.7 copy-done.1
  88.9 3.9 %apply_terms.5 = bf16[768,256]{1,0:T(8,128)(2,1)S(1)} custom-call(s32[5]{0:T(128)S(1)} %stack.11.rows_ref, s32[5]{0:T(128)S(1)} %copy-done.7, bf16[768,256]{1,0:T(8,128)(2,1)S(1)} %collective-permute-done.4.refs_0_, bf16[768,256]{1,0:T(8,128)(2,1)S(1)} %collective-permute-done.5.refs_1_, bf16[768,256]{1,0:T(8,128)(2,1)S(1)} %bitcast.16, ...), custom_call_target="tpu_custom_call" | custom-call | tf_op jit(solution)/shard_map/apply_terms/pallas_call | solution.py:81
  92.8 13.1 %all_to_all.47 = bf16[8,96,256]{2,1,0:T(8,128)(2,1)S(1)} all-to-all(bf16[8,96,256]{2,1,0:T(8,128)(2,1)S(1)} %bitcast.37), channel_id=1, replica_groups=mesh['sec'=32,'mpo'=8] {'mpo'}, dimensions={0} | all-to-all | bytes 786432 | tf_op jit(solution)/shard_map/all_to_all | solution.py:256
  106.0 13.1 %all_to_all.48 = bf16[8,96,256]{2,1,0:T(8,128)(2,1)S(1)} all-to-all(bf16[8,96,256]{2,1,0:T(8,128)(2,1)S(1)} %broadcast_in_dim.27), channel_id=1, replica_groups=mesh['sec'=32,'mpo'=8] {'mpo'}, dimensions={0} | all-to-all | bytes 786432 | tf_op jit(solution)/shard_map/all_to_all | solution.py:21
  120.1 8.9 %collective-permute-start.10 = (bf16[768,256]{1,0:T(8,128)(2,1)S(1)}, bf16[768,256]{1,0:T(8,128)(2,1)S(1)}, u32[]{:S(2)}, u32[]{:S(2)}) collective-permute-start(bf16[768,256]{1,0:T(8,128)(2,1)S(1)} %bitcast.20), channel_id=1, source_target_pairs={{0,8},{8,16},{16,24},{24,32},{32,40},{40,48},{48,56},{56,64},{64,7... | collective-permute-start | bytes 1179656 | tf_op jit(solution)/shard_map/ppermute | solution.py:28
  130.3 4.9 %collective-permute-start.8 = (bf16[768,256]{1,0:T(8,128)(2,1)S(1)}, bf16[768,256]{1,0:T(8,128)(2,1)S(1)}, u32[]{:S(2)}, u32[]{:S(2)}) collective-permute-start(bf16[768,256]{1,0:T(8,128)(2,1)S(1)} %bitcast.22), channel_id=1, source_target_pairs={{0,240},{8,248},{16,0},{24,8},{32,16},{40,24},{48,32},{56,40},{64,... | collective-permute-start | bytes 1179656 | tf_op jit(solution)/shard_map/ppermute | solution.py:28
  138.1 5.7 %collective-permute-done.8.refs_0_ = bf16[768,256]{1,0:T(8,128)(2,1)S(1)} collective-permute-done((bf16[768,256]{1,0:T(8,128)(2,1)S(1)}, bf16[768,256]{1,0:T(8,128)(2,1)S(1)}, u32[]{:S(2)}, u32[]{:S(2)}) %collective-permute-start.8) | collective-permute-done | bytes 393248 | tf_op jit(solution)/shard_map/ppermute | solution.py:28
  143.8 2.7 copy-done.2
  146.5 3.9 %apply_terms.6 = bf16[768,256]{1,0:T(8,128)(2,1)S(1)} custom-call(s32[5]{0:T(128)S(1)} %stack.11.rows_ref, s32[5]{0:T(128)S(1)} %copy-done.7, bf16[768,256]{1,0:T(8,128)(2,1)S(1)} %collective-permute-done.8.refs_0_, bf16[768,256]{1,0:T(8,128)(2,1)S(1)} %collective-permute-done.9.refs_1_, bf16[768,256]{1,0:T(8,128)(2,1)S(1)} %bitcast.23, ...), custom_call_target="tpu_custom_call" | custom-call | tf_op jit(solution)/shard_map/apply_terms/pallas_call | solution.py:81
  150.4 13.1 %all_to_all.49 = bf16[8,96,256]{2,1,0:T(8,128)(2,1)S(1)} all-to-all(bf16[8,96,256]{2,1,0:T(8,128)(2,1)S(1)} %bitcast.38), channel_id=1, replica_groups=mesh['sec'=32,'mpo'=8] {'mpo'}, dimensions={0} | all-to-all | bytes 786432 | tf_op jit(solution)/shard_map/all_to_all | solution.py:256
  163.6 13.1 %all_to_all.50 = bf16[8,96,256]{2,1,0:T(8,128)(2,1)S(1)} all-to-all(bf16[8,96,256]{2,1,0:T(8,128)(2,1)S(1)} %broadcast_in_dim.28), channel_id=1, replica_groups=mesh['sec'=32,'mpo'=8] {'mpo'}, dimensions={0} | all-to-all | bytes 786432 | tf_op jit(solution)/shard_map/all_to_all | solution.py:21
  177.6 9.1 %collective-permute-start.14 = (bf16[768,256]{1,0:T(8,128)(2,1)S(1)}, bf16[768,256]{1,0:T(8,128)(2,1)S(1)}, u32[]{:S(2)}, u32[]{:S(2)}) collective-permute-start(bf16[768,256]{1,0:T(8,128)(2,1)S(1)} %bitcast.27), channel_id=1, source_target_pairs={{0,8},{8,16},{16,24},{24,32},{32,40},{40,48},{48,56},{56,64},{64,7... | collective-permute-start | bytes 1179656 | tf_op jit(solution)/shard_map/ppermute | solution.py:28
  187.5 5.1 %collective-permute-start.12 = (bf16[768,256]{1,0:T(8,128)(2,1)S(1)}, bf16[768,256]{1,0:T(8,128)(2,1)S(1)}, u32[]{:S(2)}, u32[]{:S(2)}) collective-permute-start(bf16[768,256]{1,0:T(8,128)(2,1)S(1)} %bitcast.29), channel_id=1, source_target_pairs={{0,240},{8,248},{16,0},{24,8},{32,16},{40,24},{48,32},{56,40},{64,... | collective-permute-start | bytes 1179656 | tf_op jit(solution)/shard_map/ppermute | solution.py:28
  194.7 6.6 %collective-permute-done.12.refs_0_ = bf16[768,256]{1,0:T(8,128)(2,1)S(1)} collective-permute-done((bf16[768,256]{1,0:T(8,128)(2,1)S(1)}, bf16[768,256]{1,0:T(8,128)(2,1)S(1)}, u32[]{:S(2)}, u32[]{:S(2)}) %collective-permute-start.12) | collective-permute-done | bytes 393248 | tf_op jit(solution)/shard_map/ppermute | solution.py:28
  201.3 2.7 copy-done.3
  203.9 3.9 %apply_terms.7 = bf16[768,256]{1,0:T(8,128)(2,1)S(1)} custom-call(s32[5]{0:T(128)S(1)} %stack.11.rows_ref, s32[5]{0:T(128)S(1)} %copy-done.7, bf16[768,256]{1,0:T(8,128)(2,1)S(1)} %collective-permute-done.12.refs_0_, bf16[768,256]{1,0:T(8,128)(2,1)S(1)} %collective-permute-done.13.refs_1_, bf16[768,256]{1,0:T(8,128)(2,1)S(1)} %bitcast.30, ...), custom_call_target="tpu_custom_call" | custom-call | tf_op jit(solution)/shard_map/apply_terms/pallas_call | solution.py:81
  207.8 13.1 %all_to_all.51 = bf16[8,96,256]{2,1,0:T(8,128)(2,1)S(1)} all-to-all(bf16[8,96,256]{2,1,0:T(8,128)(2,1)S(1)} %bitcast.36), channel_id=1, replica_groups=mesh['sec'=32,'mpo'=8] {'mpo'}, dimensions={0} | all-to-all | bytes 786432 | tf_op jit(solution)/shard_map/all_to_all | solution.py:256
  221.8 3.5 %all-to-all-start.7 = ((bf16[8,96,256]{2,1,0:T(8,128)(2,1)}), bf16[8,96,256]{2,1,0:T(8,128)(2,1)S(1)}, u32[]{:S(2)}, u32[]{:S(2)}) async-start(bf16[8,96,256]{2,1,0:T(8,128)(2,1)} %broadcast_in_dim.50), calls=%async_computation.7 | async-start | bytes 786432 | tf_op jit(solution)/shard_map/all_to_all | solution.py:21
  225.8 10.1 %all-to-all-done.7 = bf16[8,96,256]{2,1,0:T(8,128)(2,1)S(1)} async-done(((bf16[8,96,256]{2,1,0:T(8,128)(2,1)}), bf16[8,96,256]{2,1,0:T(8,128)(2,1)S(1)}, u32[]{:S(2)}, u32[]{:S(2)}) %all-to-all-start.7) | async-done | bytes 393248 | tf_op jit(solution)/shard_map/all_to_all | solution.py:21
  237.1 26.9 %all-to-all-start.8 = ((f32[32,1,128]{2,1,0:T(1,128)}), f32[32,1,128]{2,1,0:T(1,128)S(1)}, u32[]{:S(2)}, u32[]{:S(2)}) async-start(f32[32,1,128]{2,1,0:T(1,128)} %broadcast_in_dim.52), calls=%async_computation.8 | async-start | bytes 32768 | tf_op jit(solution)/shard_map/all_to_all | solution.py:21
  264.7 40.0 %truncate.1 = (f32[96,256]{1,0:T(8,128)}, f32[96,256]{1,0:T(8,128)}) custom-call(s32[3]{0:T(128)S(1)} %pad_add_fusion.info_ref, f32[32,128]{1,0:T(8,128)S(1)} %bitcast.39, f32[768,256]{1,0:T(8,128)S(1)} %get-tuple-element.3.refs_0_.start_ref, bf16[768,256]{1,0:T(8,128)(2,1)S(1)} %bitcast.18, bf16[768,256]{1,0:T(8,128)(2,1)S(1)} %bitcast.25, ...), custom_call_target="tpu_custom_call" | custom-call | tf_op jit(solution)/shard_map/truncate/pallas_call | solution.py:225
  (50 shorter events, 26.4 us)
Async XLA Ops:
  2.8 83.4 %copy-start.5 = (bf16[5,256,256]{2,1,0:T(8,128)(2,1)S(1)}, bf16[5,256,256]{2,1,0:T(8,128)(2,1)}, u32[]{:S(2)}) copy-start(bf16[5,256,256]{2,1,0:T(8,128)(2,1)} %refs_6_.7) | copy-start | bytes 1966084
  4.2 82.0 %copy-start.7 = (s32[5]{0:T(128)S(1)}, s32[5]{0:T(128)}, u32[]{:S(2)}) copy-start(s32[5]{0:T(128)} %charges_ref.7) | copy-start | bytes 64
  4.2 12.7 %collective-permute-start.3 = (bf16[768,256]{1,0:T(8,128)(2,1)S(1)}, bf16[768,256]{1,0:T(8,128)(2,1)S(1)}, u32[]{:S(2)}, u32[]{:S(2)}) collective-permute-start(bf16[768,256]{1,0:T(8,128)(2,1)S(1)} %get-tuple-element.2.refs_2_), channel_id=1, source_target_pairs={{0,16},{8,24},{16,32},{24,40},{32,48},{40,56},{48,64},{56,72},{64,... | collective-permute-start | bytes 1179656 | tf_op jit(solution)/shard_map/ppermute | solution.py:28
  6.4 13.1 %collective-permute-start.2 = (bf16[768,256]{1,0:T(8,128)(2,1)S(1)}, bf16[768,256]{1,0:T(8,128)(2,1)S(1)}, u32[]{:S(2)}, u32[]{:S(2)}) collective-permute-start(bf16[768,256]{1,0:T(8,128)(2,1)S(1)} %get-tuple-element.2.refs_2_), channel_id=1, source_target_pairs={{0,8},{8,16},{16,24},{24,32},{32,40},{40,48},{48,56},{56,64},{64,7... | collective-permute-start | bytes 1179656 | tf_op jit(solution)/shard_map/ppermute | solution.py:28
  8.5 11.2 %collective-permute-start.1 = (bf16[768,256]{1,0:T(8,128)(2,1)S(1)}, bf16[768,256]{1,0:T(8,128)(2,1)S(1)}, u32[]{:S(2)}, u32[]{:S(2)}) collective-permute-start(bf16[768,256]{1,0:T(8,128)(2,1)S(1)} %get-tuple-element.2.refs_2_), channel_id=1, source_target_pairs={{0,248},{8,0},{16,8},{24,16},{32,24},{40,32},{48,40},{56,48},{64,5... | collective-permute-start | bytes 1179656 | tf_op jit(solution)/shard_map/ppermute | solution.py:28
  8.6 12.7 %collective-permute-start = (bf16[768,256]{1,0:T(8,128)(2,1)S(1)}, bf16[768,256]{1,0:T(8,128)(2,1)S(1)}, u32[]{:S(2)}, u32[]{:S(2)}) collective-permute-start(bf16[768,256]{1,0:T(8,128)(2,1)S(1)} %get-tuple-element.2.refs_2_), channel_id=1, source_target_pairs={{0,240},{8,248},{16,0},{24,8},{32,16},{40,24},{48,32},{56,40},{64,... | collective-permute-start | bytes 1179656 | tf_op jit(solution)/shard_map/ppermute | solution.py:28
  21.3 2.7 copy-start
  23.9 1.1 copy-start.4
  25.0 0.7 copy-start.6
  61.1 16.4 %collective-permute-start.7 = (bf16[768,256]{1,0:T(8,128)(2,1)S(1)}, bf16[768,256]{1,0:T(8,128)(2,1)S(1)}, u32[]{:S(2)}, u32[]{:S(2)}) collective-permute-start(bf16[768,256]{1,0:T(8,128)(2,1)S(1)} %bitcast.12), channel_id=1, source_target_pairs={{0,16},{8,24},{16,32},{24,40},{32,48},{40,56},{48,64},{56,72},{64,... | collective-permute-start | bytes 1179656 | tf_op jit(solution)/shard_map/ppermute | solution.py:28
  61.3 16.7 %collective-permute-start.6 = (bf16[768,256]{1,0:T(8,128)(2,1)S(1)}, bf16[768,256]{1,0:T(8,128)(2,1)S(1)}, u32[]{:S(2)}, u32[]{:S(2)}) collective-permute-start(bf16[768,256]{1,0:T(8,128)(2,1)S(1)} %bitcast.13), channel_id=1, source_target_pairs={{0,8},{8,16},{16,24},{24,32},{32,40},{40,48},{48,56},{56,64},{64,7... | collective-permute-start | bytes 1179656 | tf_op jit(solution)/shard_map/ppermute | solution.py:28
  70.9 8.7 %collective-permute-start.5 = (bf16[768,256]{1,0:T(8,128)(2,1)S(1)}, bf16[768,256]{1,0:T(8,128)(2,1)S(1)}, u32[]{:S(2)}, u32[]{:S(2)}) collective-permute-start(bf16[768,256]{1,0:T(8,128)(2,1)S(1)} %bitcast.14), channel_id=1, source_target_pairs={{0,248},{8,0},{16,8},{24,16},{32,24},{40,32},{48,40},{56,48},{64,5... | collective-permute-start | bytes 1179656 | tf_op jit(solution)/shard_map/ppermute | solution.py:28
  72.4 13.8 %collective-permute-start.4 = (bf16[768,256]{1,0:T(8,128)(2,1)S(1)}, bf16[768,256]{1,0:T(8,128)(2,1)S(1)}, u32[]{:S(2)}, u32[]{:S(2)}) collective-permute-start(bf16[768,256]{1,0:T(8,128)(2,1)S(1)} %bitcast.15), channel_id=1, source_target_pairs={{0,240},{8,248},{16,0},{24,8},{32,16},{40,24},{48,32},{56,40},{64,... | collective-permute-start | bytes 1179656 | tf_op jit(solution)/shard_map/ppermute | solution.py:28
  86.2 2.7 copy-start.1
  119.1 16.0 %collective-permute-start.11 = (bf16[768,256]{1,0:T(8,128)(2,1)S(1)}, bf16[768,256]{1,0:T(8,128)(2,1)S(1)}, u32[]{:S(2)}, u32[]{:S(2)}) collective-permute-start(bf16[768,256]{1,0:T(8,128)(2,1)S(1)} %bitcast.19), channel_id=1, source_target_pairs={{0,16},{8,24},{16,32},{24,40},{32,48},{40,56},{48,64},{56,72},{64,... | collective-permute-start | bytes 1179656 | tf_op jit(solution)/shard_map/ppermute | solution.py:28
  120.1 16.6 %collective-permute-start.10 = (bf16[768,256]{1,0:T(8,128)(2,1)S(1)}, bf16[768,256]{1,0:T(8,128)(2,1)S(1)}, u32[]{:S(2)}, u32[]{:S(2)}) collective-permute-start(bf16[768,256]{1,0:T(8,128)(2,1)S(1)} %bitcast.20), channel_id=1, source_target_pairs={{0,8},{8,16},{16,24},{24,32},{32,40},{40,48},{48,56},{56,64},{64,7... | collective-permute-start | bytes 1179656 | tf_op jit(solution)/shard_map/ppermute | solution.py:28
  129.0 9.1 %collective-permute-start.9 = (bf16[768,256]{1,0:T(8,128)(2,1)S(1)}, bf16[768,256]{1,0:T(8,128)(2,1)S(1)}, u32[]{:S(2)}, u32[]{:S(2)}) collective-permute-start(bf16[768,256]{1,0:T(8,128)(2,1)S(1)} %bitcast.21), channel_id=1, source_target_pairs={{0,248},{8,0},{16,8},{24,16},{32,24},{40,32},{48,40},{56,48},{64,5... | collective-permute-start | bytes 1179656 | tf_op jit(solution)/shard_map/ppermute | solution.py:28
  130.3 13.6 %collective-permute-start.8 = (bf16[768,256]{1,0:T(8,128)(2,1)S(1)}, bf16[768,256]{1,0:T(8,128)(2,1)S(1)}, u32[]{:S(2)}, u32[]{:S(2)}) collective-permute-start(bf16[768,256]{1,0:T(8,128)(2,1)S(1)} %bitcast.22), channel_id=1, source_target_pairs={{0,240},{8,248},{16,0},{24,8},{32,16},{40,24},{48,32},{56,40},{64,... | collective-permute-start | bytes 1179656 | tf_op jit(solution)/shard_map/ppermute | solution.py:28
  143.8 2.7 copy-start.2
  163.6 61.7 %copy-start.8 = (s32[32]{0:T(128)S(1)}, s32[32]{0:T(128)}, u32[]{:S(2)}) copy-start(s32[32]{0:T(128)} %param.11) | copy-start | bytes 388
  176.7 15.8 %collective-permute-start.15 = (bf16[768,256]{1,0:T(8,128)(2,1)S(1)}, bf16[768,256]{1,0:T(8,128)(2,1)S(1)}, u32[]{:S(2)}, u32[]{:S(2)}) collective-permute-start(bf16[768,256]{1,0:T(8,128)(2,1)S(1)} %bitcast.26), channel_id=1, source_target_pairs={{0,16},{8,24},{16,32},{24,40},{32,48},{40,56},{48,64},{56,72},{64,... | collective-permute-start | bytes 1179656 | tf_op jit(solution)/shard_map/ppermute | solution.py:28
  177.6 17.0 %collective-permute-start.14 = (bf16[768,256]{1,0:T(8,128)(2,1)S(1)}, bf16[768,256]{1,0:T(8,128)(2,1)S(1)}, u32[]{:S(2)}, u32[]{:S(2)}) collective-permute-start(bf16[768,256]{1,0:T(8,128)(2,1)S(1)} %bitcast.27), channel_id=1, source_target_pairs={{0,8},{8,16},{16,24},{24,32},{32,40},{40,48},{48,56},{56,64},{64,7... | collective-permute-start | bytes 1179656 | tf_op jit(solution)/shard_map/ppermute | solution.py:28
  186.7 8.0 %collective-permute-start.13 = (bf16[768,256]{1,0:T(8,128)(2,1)S(1)}, bf16[768,256]{1,0:T(8,128)(2,1)S(1)}, u32[]{:S(2)}, u32[]{:S(2)}) collective-permute-start(bf16[768,256]{1,0:T(8,128)(2,1)S(1)} %bitcast.28), channel_id=1, source_target_pairs={{0,248},{8,0},{16,8},{24,16},{32,24},{40,32},{48,40},{56,48},{64,5... | collective-permute-start | bytes 1179656 | tf_op jit(solution)/shard_map/ppermute | solution.py:28
  187.5 13.8 %collective-permute-start.12 = (bf16[768,256]{1,0:T(8,128)(2,1)S(1)}, bf16[768,256]{1,0:T(8,128)(2,1)S(1)}, u32[]{:S(2)}, u32[]{:S(2)}) collective-permute-start(bf16[768,256]{1,0:T(8,128)(2,1)S(1)} %bitcast.29), channel_id=1, source_target_pairs={{0,240},{8,248},{16,0},{24,8},{32,16},{40,24},{48,32},{56,40},{64,... | collective-permute-start | bytes 1179656 | tf_op jit(solution)/shard_map/ppermute | solution.py:28
  201.3 2.7 copy-start.3
  221.8 14.1 %all-to-all-start.7 = ((bf16[8,96,256]{2,1,0:T(8,128)(2,1)}), bf16[8,96,256]{2,1,0:T(8,128)(2,1)S(1)}, u32[]{:S(2)}, u32[]{:S(2)}) async-start(bf16[8,96,256]{2,1,0:T(8,128)(2,1)} %broadcast_in_dim.50), calls=%async_computation.7 | async-start | bytes 786432 | tf_op jit(solution)/shard_map/all_to_all | solution.py:21
  237.1 27.6 %all-to-all-start.8 = ((f32[32,1,128]{2,1,0:T(1,128)}), f32[32,1,128]{2,1,0:T(1,128)S(1)}, u32[]{:S(2)}, u32[]{:S(2)}) async-start(f32[32,1,128]{2,1,0:T(1,128)} %broadcast_in_dim.52), calls=%async_computation.8 | async-start | bytes 32768 | tf_op jit(solution)/shard_map/all_to_all | solution.py:21

commit v2 on v0

v2 whole, which is shorter than its diff:
```python
import jax
import jax.numpy as jnp
from jax import lax
from jax.experimental import pallas as pl
from jax.experimental.pallas import tpu as pltpu
from jax.sharding import PartitionSpec as P

MEAN = 256
ITERS = 4
REACH = 2
SHRINK = 2.0**-4
epsilon = 1e-06
step_size = 0.1
highest = lax.Precision.HIGHEST
TILE = 256
BASE = 64
EXTRA = 16
PAIRS = [(i, j) for i in range(ITERS + 1) for j in range(i, ITERS + 1)]
SMEM = pl.BlockSpec(memory_space=pltpu.SMEM)
VMEM = pl.BlockSpec(memory_space=pltpu.VMEM)


def call(body, name, out_shape, in_specs, scratch=(), limit=16):
    return pl.pallas_call(
        body,
        in_specs=in_specs,
        out_specs=jax.tree.map(lambda _: VMEM, out_shape),
        out_shape=out_shape,
        scratch_shapes=list(scratch),
        compiler_params=pltpu.CompilerParams(vmem_limit_bytes=limit << 20),
        name=name,
    )


def like(shape, dtype):
    return jax.ShapeDtypeStruct(shape, dtype)


def own_sector():
    return lax.axis_index("sec")


def row_index(shape, base=0):
    return base + lax.broadcasted_iota(jnp.int32, shape, len(shape) - 2)


def begin_body(block_rows_ref, guess_ref, out_ref):
    live = row_index(guess_ref.shape) < block_rows_ref[own_sector()]
    out_ref[...] = jnp.where(live, guess_ref[...], 0.0).astype(out_ref.dtype)


def begin(block_rows, guess):
    return call(begin_body, "begin", like(guess.shape, jnp.bfloat16), [SMEM, VMEM])(
        block_rows, guess
    )


def terms_body(
    block_rows_ref, charges_ref, own_ref, partner_ref, other_ref, ahead_ref, behind_ref,
    left_ref, right_ref, out_ref, held, middles,
):
    sector = own_sector()
    sectors = block_rows_ref.shape[0]
    core = lax.rem(sector, 2)
    held[0] = ahead_ref[...]
    held[2] = own_ref[...]
    held[4] = behind_ref[...]
    held[1 + 2 * core] = partner_ref[...]
    held[3 - 2 * core] = other_ref[...]
    own_rows = block_rows_ref[sector]
    terms, capacity, _ = left_ref.shape
    tiles = capacity // TILE

    def apply_term(term, _):
        charge = charges_ref[term]
        source_rows = block_rows_ref[lax.rem(sector - charge + sectors, sectors)]
        for i in range(1, tiles + 1):
            for j in range(1, tiles + 1):
                fits = (own_rows > (i - 1) * TILE) & (source_rows > (j - 1) * TILE)
                if i < tiles:
                    fits = fits & (own_rows <= i * TILE)
                if j < tiles:
                    fits = fits & (source_rows <= j * TILE)

                @pl.when(fits)
                def _():
                    middles[term, : i * TILE, :] = jnp.dot(
                        left_ref[term, : i * TILE, : j * TILE],
                        held[REACH + charge, : j * TILE, :],
                        preferred_element_type=jnp.float32,
                    ).astype(jnp.bfloat16)
        return 0

    lax.fori_loop(0, terms, apply_term, 0)
    for i in range(1, tiles + 1):
        fits = own_rows > (i - 1) * TILE
        if i < tiles:
            fits = fits & (own_rows <= i * TILE)

        @pl.when(fits)
        def _():
            high = i * TILE
            total = 0.0
            for term in range(terms):
                total = total + jnp.dot(
                    middles[term, :high, :], right_ref[term], preferred_element_type=jnp.float32
                )
            live = row_index(total.shape) < own_rows
            out_ref[:high, :] = jnp.where(live, total, 0.0).astype(out_ref.dtype)
            if high < capacity:
                out_ref[high:, :] = jnp.zeros((capacity - high, total.shape[1]), out_ref.dtype)


def apply_terms(block_rows, charges, blocks, left_env, right_env):
    terms, capacity, _ = left_env.shape
    width = right_env.shape[-1]
    return call(
        terms_body,
        "apply_terms",
        like((capacity, width), jnp.bfloat16),
        [SMEM, SMEM] + [VMEM] * 7,
        [
            pltpu.VMEM((2 * REACH + 1, capacity, width), jnp.bfloat16),
            pltpu.VMEM((terms, capacity, width), jnp.bfloat16),
        ],
    )(block_rows, charges, *blocks, left_env, right_env)


def next_slab(pieces_ref, slab):
    applied = jnp.sum(pieces_ref[...].astype(jnp.float32), axis=0)
    return (slab - step_size * applied) * SHRINK


def first_slab_body(block_rows_ref, guess_ref, pieces_ref, start_ref, new_ref, sent_ref):
    rows = start_ref.shape[0]
    base = pl.multiple_of(lax.axis_index("mpo") * rows, 8)
    slab = guess_ref[pl.ds(base, rows), :]
    slab = jnp.where(row_index(slab.shape, base) < block_rows_ref[own_sector()], slab, 0.0)
    start_ref[...] = slab
    new = next_slab(pieces_ref, slab)
    new_ref[...] = new
    sent_ref[...] = jnp.broadcast_to(new.astype(sent_ref.dtype)[None], sent_ref.shape)


def slab_body(slab_ref, pieces_ref, new_ref, sent_ref):
    new = next_slab(pieces_ref, slab_ref[...])
    new_ref[...] = new
    sent_ref[...] = jnp.broadcast_to(new.astype(sent_ref.dtype)[None], sent_ref.shape)


def last_slab_body(*refs):
    slab_refs, (pieces_ref, new_ref, sent_ref) = refs[:ITERS], refs[ITERS:]
    slabs = [ref[...] for ref in slab_refs]
    new = next_slab(pieces_ref, slabs[-1])
    new_ref[...] = new
    slabs.append(new)
    members, rows, width = pieces_ref.shape
    lane = lax.broadcasted_iota(jnp.int32, (1, width), 1)
    table = jnp.zeros((1, width), jnp.float32)
    for place, (i, j) in enumerate(PAIRS):
        value = jnp.sum(jnp.sum(slabs[i] * slabs[j], axis=0, keepdims=True), axis=1, keepdims=True)
        table = table + jnp.where(lane == place, value, 0.0)
    high = table.astype(jnp.bfloat16)
    rest = table - high.astype(jnp.float32)
    middle = rest.astype(jnp.bfloat16)
    low = (rest - middle.astype(jnp.float32)).astype(jnp.bfloat16)
    row = row_index((EXTRA, width))
    packed = jnp.where(
        row == 0,
        high.astype(jnp.float32),
        jnp.where(
            row == 1,
            middle.astype(jnp.float32),
            jnp.where(row == 2, low.astype(jnp.float32), 0.0),
        ),
    ).astype(jnp.bfloat16)
    sent_ref[:, :rows, :] = jnp.broadcast_to(new.astype(jnp.bfloat16)[None], pieces_ref.shape)
    sent_ref[:, rows:, :] = jnp.broadcast_to(packed[None], (members, EXTRA, width))


def table_body(gathered_ref, out_ref):
    rows = gathered_ref.shape[1] - EXTRA
    parts = gathered_ref[:, rows:, :].astype(jnp.float32)
    summed = jnp.sum(jnp.sum(parts, axis=0), axis=0, keepdims=True)
    out_ref[...] = jnp.broadcast_to(summed[None, :, :128], out_ref.shape)


def dot32(a, b, dims):
    return lax.dot_general(
        a, b, (dims, ((), ())), precision=highest, preferred_element_type=jnp.float32
    )


def inverse_of(block):
    size = block.shape[0]
    row = lax.broadcasted_iota(jnp.int32, block.shape, 0)
    lane = lax.broadcasted_iota(jnp.int32, block.shape, 1)
    for k in range(0, size, 2):
        row0, row1 = block[k : k + 1, :], block[k + 1 : k + 2, :]
        col0 = jnp.broadcast_to(block[:, k : k + 1], block.shape)
        col1 = jnp.broadcast_to(block[:, k + 1 : k + 2], block.shape)
        a, b, d = col0[k : k + 1, :], col0[k + 1 : k + 2, :], col1[k + 1 : k + 2, :]
        scale = 1.0 / (a * d - b * b)
        at0, at1 = lane[:1] == k, lane[:1] == k + 1
        row0 = jnp.where(at0, -1.0, jnp.where(at1, 0.0, row0))
        row1 = jnp.where(at1, -1.0, jnp.where(at0, 0.0, row1))
        new0 = (d * scale) * row0 - (b * scale) * row1
        new1 = (a * scale) * row1 - (b * scale) * row0
        rest = jnp.where((lane == k) | (lane == k + 1), 0.0, block) - col0 * new0 - col1 * new1
        block = jnp.where(row == k, new0, jnp.where(row == k + 1, new1, rest))
    return -block


def weights_of(sums_ref):
    sectors = sums_ref.shape[0]
    summed = jnp.sum(sums_ref[...], axis=0)
    table = {}
    for place, (i, j) in enumerate(PAIRS):
        table[i, j] = table[j, i] = summed[:, place : place + 1]

    def inner(a, b):
        out = 0.0
        for i, x in enumerate(a):
            for j, y in enumerate(b):
                out = out + x * y * table[i, j]
        return out

    entries = float(MEAN * sectors * 256)

    def scale_of(squares):
        return lax.rsqrt(squares / entries + epsilon)

    weights = [scale_of(table[0, 0])]
    for _ in range(ITERS):
        up = [0.0 * weights[0]] + [x * (1.0 / SHRINK) for x in weights]
        padded = weights + [0.0 * weights[0]]
        image = [(x - y) * (1.0 / step_size) for x, y in zip(padded, up)]
        rayleigh = inner(weights, image) / (inner(weights, weights) + epsilon)
        update = [y + step_size * rayleigh * x for x, y in zip(padded, up)]
        scale = scale_of(jnp.maximum(inner(update, update), 0.0))
        weights = [x * scale for x in update]
    return weights


def truncate_body(block_rows_ref, ranks_ref, sums_ref, guess_ref, *refs):
    powers = refs[:ITERS]
    slabs = refs[ITERS : 2 * ITERS + 1]
    slab_ref, cut_ref, gram = refs[2 * ITERS + 1 :]
    sector = own_sector()
    weights = weights_of(sums_ref)
    slab_rows, width = slab_ref.shape
    live = row_index(guess_ref.shape) < block_rows_ref[sector]
    current = jnp.where(live, guess_ref[...], 0.0) * weights[0]
    for weight, ref in zip(weights[1:], powers):
        power = ref[...] if len(ref.shape) == 2 else ref[:, :slab_rows, :].reshape(current.shape)
        current = current + weight * power.astype(jnp.float32)
    density = dot32(current, current, ((0,), (0,)))
    row = lax.broadcasted_iota(jnp.int32, density.shape, 0)
    lane = lax.broadcasted_iota(jnp.int32, density.shape, 1)
    diagonal = (row == lane).astype(jnp.float32)
    kept = lane < ranks_ref[sector]
    basis = jnp.where(kept, diagonal + density * (1.0 / MEAN), 0.0)
    gram[...] = dot32(basis, basis, ((0,), (0,))) + jnp.where(kept, 0.0, diagonal)
    panel_row = lax.broadcasted_iota(jnp.int32, (BASE, width), 0)
    panel_lane = lax.broadcasted_iota(jnp.int32, (BASE, width), 1)
    for low in range(0, width, BASE):
        panel = gram[low : low + BASE, :]
        inverse = inverse_of(panel[:, low : low + BASE])
        inside = (panel_lane >= low) & (panel_lane < low + BASE)
        select = (panel_lane == panel_row + low).astype(jnp.float32)
        rest = jnp.where(inside, 0.0, panel)
        solved = dot32(inverse, rest, ((1,), (0,)))
        change = dot32(
            jnp.concatenate([rest, solved], axis=0),
            jnp.concatenate([solved, -select], axis=0),
            ((0,), (0,)),
        )
        taken = (lane >= low) & (lane < low + BASE)
        gram[...] = jnp.where(taken, 0.0, gram[...]) - change
        gram[low : low + BASE, :] = solved - dot32(inverse, select, ((1,), (0,)))
    slab = weights[0] * slabs[0][...]
    for weight, ref in zip(weights[1:], slabs[1:]):
        slab = slab + weight * ref[...]
    slab_ref[...] = slab
    coords = dot32(slab, basis, ((1,), (0,)))
    solved = -dot32(coords, gram[...], ((1,), (0,)))
    cut_ref[...] = dot32(solved, basis, ((1,), (1,)))


def passed_along(array, by):
    peers = lax.axis_size("sec")
    return lax.ppermute(array, "sec", [(i, (i + by) % peers) for i in range(peers)])


def swapped(array):
    peers = lax.axis_size("sec")
    return lax.ppermute(array, "sec", [(i, i ^ 1) for i in range(peers)])


def neighbours(whole):
    ahead, behind = passed_along(whole, -2), passed_along(whole, 2)
    whole, ahead, behind = lax.optimization_barrier((whole, ahead, behind))
    partner = swapped(whole)
    other = swapped(jnp.where(own_sector() % 2 == 0, ahead, behind))
    return whole, partner, other, ahead, behind


def shards(guess, left_env, right_env, block_rows, charges, ranks):
    capacity, width = guess.shape
    sectors = block_rows.shape[0]
    members = lax.axis_size("mpo")
    rows = capacity // members
    exact = like((rows, width), jnp.float32)
    sent = like((members, rows, width), jnp.bfloat16)
    sent_last = like((members, rows + EXTRA, width), jnp.bfloat16)

    def exchanged(array, axis):
        return lax.all_to_all(array, axis, 0, 0, tiled=True)

    whole = begin(block_rows, guess)
    powers, slabs = [], []
    for repeat in range(ITERS):
        part = apply_terms(block_rows, charges, neighbours(whole), left_env, right_env)
        pieces = exchanged(part.reshape(members, rows, width), "mpo")
        if repeat == 0:
            start, new, outgoing = call(
                first_slab_body, "first_slab", (exact, exact, sent), [SMEM, VMEM, VMEM]
            )(block_rows, guess, pieces)
            slabs.append(start)
        elif repeat < ITERS - 1:
            new, outgoing = call(slab_body, "slab", (exact, sent), [VMEM] * 2)(slabs[-1], pieces)
        else:
            new, outgoing = call(
                last_slab_body, "last_slab", (exact, sent_last), [VMEM] * (ITERS + 1)
            )(*slabs, pieces)
        slabs.append(new)
        gathered = exchanged(outgoing, "mpo")
        whole = gathered.reshape(capacity, width) if repeat < ITERS - 1 else gathered
        powers.append(whole)
    tables = call(table_body, "table", like((sectors, 1, 128), jnp.float32), [VMEM])(powers[-1])
    sums = exchanged(tables, "sec")
    return call(
        truncate_body,
        "truncate",
        (exact, exact),
        [SMEM, SMEM] + [VMEM] * (3 + 2 * ITERS),
        [pltpu.VMEM((width, width), jnp.float32)],
        limit=24,
    )(block_rows, ranks, sums, guess, *powers, *slabs)


def solution(mesh):
    return jax.shard_map(
        shards,
        mesh=mesh,
        in_specs=(P("sec", None), P("mpo", "sec", None), P("mpo", "sec", None), P(), P("mpo"), P()),
        out_specs=(P(("sec", "mpo"), None), P(("sec", "mpo"), None)),
        check_vma=False,
    )
```

time: 691 us -> 273 us (0.40); the launches traced: 681 us -> 271 us
  waiting for transfers between devices: 179 us -> 41 us
  blocking collectives: 275 us -> 156 us
  other arithmetic: 78.8 us -> 0.17 us
  local copies, waits for them, and re-layouts: 40.2 us -> 6.88 us
  Pallas kernels: 0 us -> 32 us
  starting transfers between devices: 65.5 us -> 34.6 us
  matrix products: 27.9 us -> 0 us
  between operations: 14.7 us -> 0.77 us
    all_to_all x10 -> x0, waiting for transfers between devices: 119 us -> none  [sent_to_all(): lax.all_to_all(jnp.broadcast_to(array[None], (peers, *array.shape)), axis...]
    all_to_all x7 -> x9, blocking collectives: 275 us -> 156 us  [exchanged(): return lax.all_to_all(array, axis, 0, 0, tiled=True)]
    another operation x9 -> x0, other arithmetic: 54 us -> none  [the longest x6 34.3 us: shards(): factor = jnp.linalg.cholesky(gram_matrix)]
    all_to_all x10 -> x0, starting transfers between devices: 41.9 us -> none  [sent_to_all(): lax.all_to_all(jnp.broadcast_to(array[None], (peers, *array.shape)), axis...]
    pallas_call x0 -> x11, Pallas kernels: none -> 32 us  [the longest x1 20.3 us: shards(): call(truncate_body, 'truncate', (exact, exact), [SMEM, SMEM] + [VMEM] * (...]
    dot_general x8 -> x0, matrix products: 26.1 us -> none  [the longest x4 22.7 us: apply_operator(): jnp.einsum('tik,tkl->til', middle, right_env, preferred_element_type=jnp....]
    reduce_sum x24 -> x0, other arithmetic: 20.3 us -> none  [the longest x13 8.57 us: of_everyone(): return sent_to_all(array, axis).sum(axis=0)]
    ppermute x16, waiting for transfers between devices: 59.8 us -> 41 us  [the longest x8 33.8 us: passed_along(): lax.ppermute(array, 'sec', [(i, (i + by) % peers) for i in range(peers)])]
  transfers between devices with their start and end apart: 26 -> 16, of which waited for: 21 -> 12; matrix products, arithmetic and copies ran while one was open for 2% -> 0% of each run, Pallas kernels for 0% -> 0%
where the time goes in v2:
time: 273 us; the launch traced here: 271 us
  blocking collectives  156 us (57%)
  waiting for transfers between devices  41 us (15%)
  starting transfers between devices  34.6 us (13%)
  Pallas kernels  32 us (12%)
  local copies, waits for them, and re-layouts  6.88 us (3%)
    all_to_all x9, blocking collectives, exchanged(): return lax.all_to_all(array, axis, 0, 0, tiled=True)  156 us
    ppermute x8, waiting for transfers between devices, passed_along(): lax.ppermute(array, 'sec', [(i, (i + by) % peers) for i in range(peers)])  33.8 us
    ppermute x8, starting transfers between devices, passed_along(): lax.ppermute(array, 'sec', [(i, (i + by) % peers) for i in range(peers)])  27.4 us
    pallas_call x1, Pallas kernels, shards(): call(truncate_body, 'truncate', (exact, exact), [SMEM, SMEM] + [VMEM] * (...  20.3 us
    pallas_call x4, Pallas kernels, apply_terms(): call(terms_body, 'apply_terms', like((capacity, width), jnp.bfloat16), [S...  9.99 us
    ppermute x8, waiting for transfers between devices, swapped(): return lax.ppermute(array, 'sec', [(i, i ^ 1) for i in range(peers)])  7.24 us
    ppermute x8, starting transfers between devices, swapped(): return lax.ppermute(array, 'sec', [(i, i ^ 1) for i in range(peers)])  7.17 us
    unnamed x24, local copies, waits for them, and re-layouts  6.88 us
  transfers between devices with their start and end apart: 16, of which 12 were waited for; matrix products, arithmetic and copies ran while one was open for 0% of the time, Pallas kernels for 0%

profile of v2, /device:TPU:1, one launch (start us, length us, event | category | flops | bytes accessed | tf_op | source)
XLA Modules:
  0.0 271.4 jit_solution(14313379645439314608)
XLA Ops:
  3.0 2.2 collective-permute-start.1
  5.2 3.7 %collective-permute-start = (bf16[768,256]{1,0:T(8,128)(2,1)S(1)}, bf16[768,256]{1,0:T(8,128)(2,1)S(1)}, u32[]{:S(2)}, u32[]{:S(2)}) collective-permute-start(bf16[768,256]{1,0:T(8,128)(2,1)S(1)} %begin.1.own_ref), channel_id=1, source_target_pairs={{0,240},{8,248},{16,0},{24,8},{32,16},{40,24},{48,32},{56,40},{64,... | collective-permute-start | bytes 1179656 | tf_op jit(solution)/shard_map/ppermute | solution.py:292
  9.0 6.8 %collective-permute-done.1.behind_ref = bf16[768,256]{1,0:T(8,128)(2,1)S(1)} collective-permute-done((bf16[768,256]{1,0:T(8,128)(2,1)S(1)}, bf16[768,256]{1,0:T(8,128)(2,1)S(1)}, u32[]{:S(2)}, u32[]{:S(2)}) %collective-permute-start.1) | collective-permute-done | bytes 393248 | tf_op jit(solution)/shard_map/ppermute | solution.py:292
  15.8 3.3 %collective-permute-start.3 = (bf16[768,256]{1,0:T(8,128)(2,1)S(1)}, bf16[768,256]{1,0:T(8,128)(2,1)S(1)}, u32[]{:S(2)}, u32[]{:S(2)}) collective-permute-start(bf16[768,256]{1,0:T(8,128)(2,1)S(1)} %broadcast_select_fusion.3), channel_id=1, source_target_pairs={{0,8},{8,0},{16,24},{24,16},{32,40},{40,32},{48,56},{56,48},{64,72... | collective-permute-start | bytes 1179656 | tf_op jit(solution)/shard_map/ppermute | solution.py:297
  19.2 1.2 collective-permute-done.3.other_ref
  21.0 2.7 copy-done
  26.1 2.4 apply_terms.4
  28.5 21.9 %all_to_all.45.pieces_ref = bf16[8,96,256]{2,1,0:T(8,128)(2,1)S(1)} all-to-all(bf16[8,96,256]{2,1,0:T(8,128)(2,1)S(1)} %bitcast.22), channel_id=1, replica_groups=mesh['sec'=32,'mpo'=8] {'mpo'}, dimensions={0} | all-to-all | bytes 786432 | tf_op jit(solution)/shard_map/all_to_all | solution.py:318
  51.0 14.9 %all_to_all.46 = bf16[8,96,256]{2,1,0:T(8,128)(2,1)S(1)} all-to-all(bf16[8,96,256]{2,1,0:T(8,128)(2,1)S(1)} %get-tuple-element.28), channel_id=1, replica_groups=mesh['sec'=32,'mpo'=8] {'mpo'}, dimensions={0} | all-to-all | bytes 786432 | tf_op jit(solution)/shard_map/all_to_all | solution.py:318
  65.9 9.3 %collective-permute-start.4 = (bf16[768,256]{1,0:T(8,128)(2,1)S(1)}, bf16[768,256]{1,0:T(8,128)(2,1)S(1)}, u32[]{:S(2)}, u32[]{:S(2)}) collective-permute-start(bf16[768,256]{1,0:T(8,128)(2,1)S(1)} %bitcast.8), channel_id=1, source_target_pairs={{0,240},{8,248},{16,0},{24,8},{32,16},{40,24},{48,32},{56,40},{64,... | collective-permute-start | bytes 1179656 | tf_op jit(solution)/shard_map/ppermute | solution.py:292
  75.1 9.0 %collective-permute-done.5.behind_ref = bf16[768,256]{1,0:T(8,128)(2,1)S(1)} collective-permute-done((bf16[768,256]{1,0:T(8,128)(2,1)S(1)}, bf16[768,256]{1,0:T(8,128)(2,1)S(1)}, u32[]{:S(2)}, u32[]{:S(2)}) %collective-permute-start.5) | collective-permute-done | bytes 393248 | tf_op jit(solution)/shard_map/ppermute | solution.py:292
  84.2 1.2 collective-permute-start.7
  85.4 1.2 collective-permute-done.7.other_ref
  87.3 2.6 apply_terms.5
  89.8 17.5 %all_to_all.47.pieces_ref = bf16[8,96,256]{2,1,0:T(8,128)(2,1)S(1)} all-to-all(bf16[8,96,256]{2,1,0:T(8,128)(2,1)S(1)} %bitcast.23), channel_id=1, replica_groups=mesh['sec'=32,'mpo'=8] {'mpo'}, dimensions={0} | all-to-all | bytes 786432 | tf_op jit(solution)/shard_map/all_to_all | solution.py:318
  107.5 16.7 %all_to_all.48 = bf16[8,96,256]{2,1,0:T(8,128)(2,1)S(1)} all-to-all(bf16[8,96,256]{2,1,0:T(8,128)(2,1)S(1)} %get-tuple-element.33), channel_id=1, replica_groups=mesh['sec'=32,'mpo'=8] {'mpo'}, dimensions={0} | all-to-all | bytes 786432 | tf_op jit(solution)/shard_map/all_to_all | solution.py:318
  124.2 6.1 %collective-permute-start.8 = (bf16[768,256]{1,0:T(8,128)(2,1)S(1)}, bf16[768,256]{1,0:T(8,128)(2,1)S(1)}, u32[]{:S(2)}, u32[]{:S(2)}) collective-permute-start(bf16[768,256]{1,0:T(8,128)(2,1)S(1)} %bitcast.13), channel_id=1, source_target_pairs={{0,240},{8,248},{16,0},{24,8},{32,16},{40,24},{48,32},{56,40},{64,... | collective-permute-start | bytes 1179656 | tf_op jit(solution)/shard_map/ppermute | solution.py:292
  130.3 9.0 %collective-permute-done.9.behind_ref = bf16[768,256]{1,0:T(8,128)(2,1)S(1)} collective-permute-done((bf16[768,256]{1,0:T(8,128)(2,1)S(1)}, bf16[768,256]{1,0:T(8,128)(2,1)S(1)}, u32[]{:S(2)}, u32[]{:S(2)}) %collective-permute-start.9) | collective-permute-done | bytes 393248 | tf_op jit(solution)/shard_map/ppermute | solution.py:292
  139.3 1.2 collective-permute-start.11
  140.6 1.2 collective-permute-done.11.other_ref
  142.4 2.4 apply_terms.6
  144.8 17.5 %all_to_all.49.pieces_ref = bf16[8,96,256]{2,1,0:T(8,128)(2,1)S(1)} all-to-all(bf16[8,96,256]{2,1,0:T(8,128)(2,1)S(1)} %bitcast.24), channel_id=1, replica_groups=mesh['sec'=32,'mpo'=8] {'mpo'}, dimensions={0} | all-to-all | bytes 786432 | tf_op jit(solution)/shard_map/all_to_all | solution.py:318
  162.4 16.7 %all_to_all.50 = bf16[8,96,256]{2,1,0:T(8,128)(2,1)S(1)} all-to-all(bf16[8,96,256]{2,1,0:T(8,128)(2,1)S(1)} %get-tuple-element.38), channel_id=1, replica_groups=mesh['sec'=32,'mpo'=8] {'mpo'}, dimensions={0} | all-to-all | bytes 786432 | tf_op jit(solution)/shard_map/all_to_all | solution.py:318
  179.2 6.1 %collective-permute-start.12 = (bf16[768,256]{1,0:T(8,128)(2,1)S(1)}, bf16[768,256]{1,0:T(8,128)(2,1)S(1)}, u32[]{:S(2)}, u32[]{:S(2)}) collective-permute-start(bf16[768,256]{1,0:T(8,128)(2,1)S(1)} %bitcast.18), channel_id=1, source_target_pairs={{0,240},{8,248},{16,0},{24,8},{32,16},{40,24},{48,32},{56,40},{64,... | collective-permute-start | bytes 1179656 | tf_op jit(solution)/shard_map/ppermute | solution.py:292
  185.3 9.0 %collective-permute-done.13.behind_ref = bf16[768,256]{1,0:T(8,128)(2,1)S(1)} collective-permute-done((bf16[768,256]{1,0:T(8,128)(2,1)S(1)}, bf16[768,256]{1,0:T(8,128)(2,1)S(1)}, u32[]{:S(2)}, u32[]{:S(2)}) %collective-permute-start.13) | collective-permute-done | bytes 393248 | tf_op jit(solution)/shard_map/ppermute | solution.py:292
  194.3 1.2 collective-permute-start.15
  195.6 1.2 collective-permute-done.15.other_ref
  197.4 2.6 apply_terms.7
  200.0 17.5 %all_to_all.51.refs_4_ = bf16[8,96,256]{2,1,0:T(8,128)(2,1)S(1)} all-to-all(bf16[8,96,256]{2,1,0:T(8,128)(2,1)S(1)} %bitcast.25), channel_id=1, replica_groups=mesh['sec'=32,'mpo'=8] {'mpo'}, dimensions={0} | all-to-all | bytes 786432 | tf_op jit(solution)/shard_map/all_to_all | solution.py:318
  217.9 18.8 %all_to_all.52.gathered_ref.refs_3_ = bf16[8,112,256]{2,1,0:T(8,128)(2,1)S(1)} all-to-all(bf16[8,112,256]{2,1,0:T(8,128)(2,1)S(1)} %get-tuple-element.42), channel_id=1, replica_groups=mesh['sec'=32,'mpo'=8] {'mpo'}, dimensions={0} | all-to-all | bytes 917504 | tf_op jit(solution)/shard_map/all_to_all | solution.py:318
  236.8 14.4 %all_to_all.53.sums_ref = f32[32,1,128]{2,1,0:T(1,128)S(1)} all-to-all(f32[32,1,128]{2,1,0:T(1,128)S(1)} %table.1), channel_id=1, replica_groups=mesh['sec'=32,'mpo'=8] {'sec'}, dimensions={0} | all-to-all | bytes 32768 | tf_op jit(solution)/shard_map/all_to_all | solution.py:318
  251.2 20.3 %truncate.1 = (f32[96,256]{1,0:T(8,128)}, f32[96,256]{1,0:T(8,128)}) custom-call(s32[32]{0:T(128)S(1)} %copy-done.8, s32[32]{0:T(128)S(1)} %copy-done.11, f32[32,1,128]{2,1,0:T(1,128)S(1)} %all_to_all.53.sums_ref, f32[768,256]{1,0:T(8,128)S(1)} %copy-done.5, bf16[768,256]{1,0:T(8,128)(2,1)S(1)} %bitcast.11, bf16[768,256]{1,0:T(8,128)(2,1)S(1)} %bitcast.16, ...), custom_call_target="tpu_custom_call" | custom-call | tf_op jit(solution)/shard_map/truncate/pallas_call | solution.py:342
  (48 shorter events, 8.8 us)
Async XLA Ops:
  0.6 1.1 copy-start.4
  1.8 0.7 copy-start.6
  2.4 47.9 %copy-start.5 = (f32[768,256]{1,0:T(8,128)S(1)}, f32[768,256]{1,0:T(8,128)}, u32[]{:S(2)}) copy-start(f32[768,256]{1,0:T(8,128)} %guess_ref.5) | copy-start | bytes 2359300
  3.0 12.7 %collective-permute-start.1 = (bf16[768,256]{1,0:T(8,128)(2,1)S(1)}, bf16[768,256]{1,0:T(8,128)(2,1)S(1)}, u32[]{:S(2)}, u32[]{:S(2)}) collective-permute-start(bf16[768,256]{1,0:T(8,128)(2,1)S(1)} %begin.1.own_ref), channel_id=1, source_target_pairs={{0,16},{8,24},{16,32},{24,40},{32,48},{40,56},{48,64},{56,72},{64,... | collective-permute-start | bytes 1179656 | tf_op jit(solution)/shard_map/ppermute | solution.py:292
  5.2 10.5 %collective-permute-start = (bf16[768,256]{1,0:T(8,128)(2,1)S(1)}, bf16[768,256]{1,0:T(8,128)(2,1)S(1)}, u32[]{:S(2)}, u32[]{:S(2)}) collective-permute-start(bf16[768,256]{1,0:T(8,128)(2,1)S(1)} %begin.1.own_ref), channel_id=1, source_target_pairs={{0,240},{8,248},{16,0},{24,8},{32,16},{40,24},{48,32},{56,40},{64,... | collective-permute-start | bytes 1179656 | tf_op jit(solution)/shard_map/ppermute | solution.py:292
  15.8 71.5 %copy-start.3 = (bf16[5,256,256]{2,1,0:T(8,128)(2,1)S(1)}, bf16[5,256,256]{2,1,0:T(8,128)(2,1)}, u32[]{:S(2)}) copy-start(bf16[5,256,256]{2,1,0:T(8,128)(2,1)} %right_ref.7) | copy-start | bytes 1966084
  15.8 71.5 %copy-start.10 = (s32[5]{0:T(128)S(1)}, s32[5]{0:T(128)}, u32[]{:S(2)}) copy-start(s32[5]{0:T(128)} %charges_ref.7) | copy-start | bytes 64
  15.8 4.6 %collective-permute-start.3 = (bf16[768,256]{1,0:T(8,128)(2,1)S(1)}, bf16[768,256]{1,0:T(8,128)(2,1)S(1)}, u32[]{:S(2)}, u32[]{:S(2)}) collective-permute-start(bf16[768,256]{1,0:T(8,128)(2,1)S(1)} %broadcast_select_fusion.3), channel_id=1, source_target_pairs={{0,8},{8,0},{16,24},{24,16},{32,40},{40,32},{48,56},{56,48},{64,72... | collective-permute-start | bytes 1179656 | tf_op jit(solution)/shard_map/ppermute | solution.py:297
  19.1 1.9 collective-permute-start.2
  21.0 2.7 copy-start
  23.7 1.1 copy-start.2
  24.8 0.7 copy-start.7
  25.4 0.7 copy-start.9
  26.1 61.2 %copy-start.1 = (bf16[5,768,768]{2,1,0:T(8,128)(2,1)S(1)}, bf16[5,768,768]{2,1,0:T(8,128)(2,1)}, u32[]{:S(2)}) copy-start(bf16[5,768,768]{2,1,0:T(8,128)(2,1)} %left_ref.7) | copy-start | bytes 17694724
  65.9 18.2 %collective-permute-start.5 = (bf16[768,256]{1,0:T(8,128)(2,1)S(1)}, bf16[768,256]{1,0:T(8,128)(2,1)S(1)}, u32[]{:S(2)}, u32[]{:S(2)}) collective-permute-start(bf16[768,256]{1,0:T(8,128)(2,1)S(1)} %bitcast.7), channel_id=1, source_target_pairs={{0,16},{8,24},{16,32},{24,40},{32,48},{40,56},{48,64},{56,72},{64,... | collective-permute-start | bytes 1179656 | tf_op jit(solution)/shard_map/ppermute | solution.py:292
  65.9 18.2 %collective-permute-start.4 = (bf16[768,256]{1,0:T(8,128)(2,1)S(1)}, bf16[768,256]{1,0:T(8,128)(2,1)S(1)}, u32[]{:S(2)}, u32[]{:S(2)}) collective-permute-start(bf16[768,256]{1,0:T(8,128)(2,1)S(1)} %bitcast.8), channel_id=1, source_target_pairs={{0,240},{8,248},{16,0},{24,8},{32,16},{40,24},{48,32},{56,40},{64,... | collective-permute-start | bytes 1179656 | tf_op jit(solution)/shard_map/ppermute | solution.py:292
  84.2 2.5 collective-permute-start.7
  85.3 1.9 collective-permute-start.6
  124.2 15.1 %collective-permute-start.9 = (bf16[768,256]{1,0:T(8,128)(2,1)S(1)}, bf16[768,256]{1,0:T(8,128)(2,1)S(1)}, u32[]{:S(2)}, u32[]{:S(2)}) collective-permute-start(bf16[768,256]{1,0:T(8,128)(2,1)S(1)} %bitcast.12), channel_id=1, source_target_pairs={{0,16},{8,24},{16,32},{24,40},{32,48},{40,56},{48,64},{56,72},{64,... | collective-permute-start | bytes 1179656 | tf_op jit(solution)/shard_map/ppermute | solution.py:292
  124.2 15.1 %collective-permute-start.8 = (bf16[768,256]{1,0:T(8,128)(2,1)S(1)}, bf16[768,256]{1,0:T(8,128)(2,1)S(1)}, u32[]{:S(2)}, u32[]{:S(2)}) collective-permute-start(bf16[768,256]{1,0:T(8,128)(2,1)S(1)} %bitcast.13), channel_id=1, source_target_pairs={{0,240},{8,248},{16,0},{24,8},{32,16},{40,24},{48,32},{56,40},{64,... | collective-permute-start | bytes 1179656 | tf_op jit(solution)/shard_map/ppermute | solution.py:292
  139.3 2.5 collective-permute-start.11
  140.5 1.9 collective-permute-start.10
  179.2 15.1 %collective-permute-start.13 = (bf16[768,256]{1,0:T(8,128)(2,1)S(1)}, bf16[768,256]{1,0:T(8,128)(2,1)S(1)}, u32[]{:S(2)}, u32[]{:S(2)}) collective-permute-start(bf16[768,256]{1,0:T(8,128)(2,1)S(1)} %bitcast.17), channel_id=1, source_target_pairs={{0,16},{8,24},{16,32},{24,40},{32,48},{40,56},{48,64},{56,72},{64,... | collective-permute-start | bytes 1179656 | tf_op jit(solution)/shard_map/ppermute | solution.py:292
  179.2 15.1 %collective-permute-start.12 = (bf16[768,256]{1,0:T(8,128)(2,1)S(1)}, bf16[768,256]{1,0:T(8,128)(2,1)S(1)}, u32[]{:S(2)}, u32[]{:S(2)}) collective-permute-start(bf16[768,256]{1,0:T(8,128)(2,1)S(1)} %bitcast.18), channel_id=1, source_target_pairs={{0,240},{8,248},{16,0},{24,8},{32,16},{40,24},{48,32},{56,40},{64,... | collective-permute-start | bytes 1179656 | tf_op jit(solution)/shard_map/ppermute | solution.py:292
  194.3 56.8 %copy-start.8 = (s32[32]{0:T(128)S(1)}, s32[32]{0:T(128)}, u32[]{:S(2)}) copy-start(s32[32]{0:T(128)} %block_rows_ref.13) | copy-start | bytes 388
  194.3 56.8 %copy-start.11 = (s32[32]{0:T(128)S(1)}, s32[32]{0:T(128)}, u32[]{:S(2)}) copy-start(s32[32]{0:T(128)} %ranks_ref.1) | copy-start | bytes 388
  194.3 2.5 collective-permute-start.15
  195.5 1.9 collective-permute-start.14
